TPU v7x, 32 devices: a whole 2x2x4 slice. The times are simulated.
32 devices in a mesh: dp: 4 (over z), expert: 8 (over y, x, core).
Axes of the slice: x: 2, y: 2, z: 4, core: 2. Of those that a mesh axis runs over, the one named last changes fastest.
Arguments:
- tokens: bfloat16 [4096, 1536], P(('dp', 'expert')), may hold values from -6 to 6
- routes: int32 [4096, 2], P(('dp', 'expert')), may hold values from 0 to 7, all different within a row; in each aligned block of 128 rows (0 to 127, 128 to 255, ...) at most 40 rows name the same one
- combine: float32 [4096, 2], P(('dp', 'expert')), may hold values from 0.1 to 1
- w_gate: bfloat16 [8, 1536, 1536], P('expert', None, 'dp'), may hold values from -0.15625 to 0.15625
- w_up: bfloat16 [8, 1536, 1536], P('expert', None, 'dp'), may hold values from -0.15625 to 0.15625
- w_down: bfloat16 [8, 1536, 1536], P('expert', 'dp'), may hold values from -0.15625 to 0.15625
- cotangent: bfloat16 [4096, 1536], P(('dp', 'expert')), may hold values from -2 to 2
Outputs:
- out: bfloat16 [4096, 1536], P(('dp', 'expert'))
- d_tokens: bfloat16 [4096, 1536], P(('dp', 'expert'))
- d_combine: float32 [4096, 2], P(('dp', 'expert'))
- grad_gate: bfloat16 [8, 1536, 1536], P('expert', None, 'dp')
- grad_up: bfloat16 [8, 1536, 1536], P('expert', None, 'dp')
- grad_down: bfloat16 [8, 1536, 1536], P('expert', 'dp')
Inputs may be any that keep to these rules, and one draw needn't show every extreme that they name: `routes`: the two experts of a token differ. Among the 128 tokens of one source block no expert is named more than 40 times, and in every draw some expert is named exactly 40 times by some source block.
All inputs are finite; a program needn't handle non-finite values.
Results may differ from a plain program's by a relative error of at most 0.013.
Values may be sent and summed in bfloat16 or wider, within the bound.
A program may use at most 128 MiB of HBM per device.

v0:
```python
import jax
import jax.numpy as jnp
from jax import lax
from jax.sharding import PartitionSpec as P


def dot_plain(left, right):
    return jnp.dot(left, right, preferred_element_type=jnp.float32)


def dot_last(left, right):
    return lax.dot_general(
        left, right, (((1,), (1,)), ((), ())), preferred_element_type=jnp.float32
    )


def dot_first(left, right):
    return lax.dot_general(
        left, right, (((0,), (0,)), ((), ())), preferred_element_type=jnp.float32
    )


def group_total(left, right, groups):
    left_groups = left.reshape(groups, -1, left.shape[1])
    right_groups = right.reshape(groups, -1, right.shape[1])
    part = jnp.einsum("gri,grj->gij", left_groups, right_groups, preferred_element_type=jnp.float32)
    part = lax.optimization_barrier(part.astype(jnp.bfloat16)).astype(jnp.float32)
    return jnp.sum(part, axis=0).astype(jnp.bfloat16)


def gate_grads(d_hidden, gate_pre, up_pre, sigmoid_gate):
    d_gate = (d_hidden * up_pre * sigmoid_gate * (1.0 + gate_pre * (1.0 - sigmoid_gate))).astype(
        jnp.bfloat16
    )
    d_up = (d_hidden * gate_pre * sigmoid_gate).astype(jnp.bfloat16)
    return (d_gate, d_up)


def on_device(tokens, routes, combine, w_gate, w_up, w_down, cotangent):
    experts = lax.axis_size("expert")
    groups = lax.axis_size("dp")
    count = tokens.shape[0]
    width = tokens.shape[1]
    capacity = 10 * count // (4 * experts)
    slot_total = experts * capacity
    flat = routes.reshape(-1)
    onehot = (flat[:, None] == jnp.arange(experts, dtype=jnp.int32)[None, :]).astype(jnp.int32)
    before = jnp.cumsum(onehot, axis=0) - onehot
    target_row = (flat * capacity + jnp.sum(before * onehot, axis=1)).reshape(count, 2)
    positions = jnp.arange(slot_total, dtype=jnp.int32)[:, None]
    pick_first = (positions == target_row[None, :, 0]).astype(jnp.bfloat16)
    pick_second = (positions == target_row[None, :, 1]).astype(jnp.bfloat16)
    pick_both = pick_first + pick_second
    send_rows = dot_plain(pick_both, tokens).astype(jnp.bfloat16).reshape(experts, capacity, width)
    token_rows = lax.all_to_all(
        send_rows, "expert", split_axis=0, concat_axis=0, tiled=True
    ).reshape(slot_total, width)
    local_gate = w_gate[0]
    local_up = w_up[0]
    local_down = w_down[0]
    group_rows = lax.all_gather(token_rows, "dp", axis=0, tiled=True)
    gate_pre = dot_plain(group_rows, local_gate)
    up_pre = dot_plain(group_rows, local_up)
    sigmoid_gate = jax.nn.sigmoid(gate_pre)
    hidden = (gate_pre * sigmoid_gate * up_pre).astype(jnp.bfloat16)
    expert_out = lax.psum_scatter(
        dot_plain(hidden, local_down).astype(jnp.bfloat16), "dp", scatter_dimension=0, tiled=True
    )
    returned = lax.all_to_all(
        expert_out.reshape(experts, capacity, width),
        "expert",
        split_axis=0,
        concat_axis=0,
        tiled=True,
    ).reshape(slot_total, width)
    first_out = dot_first(pick_first, returned)
    second_out = dot_first(pick_second, returned)
    out = (combine[:, 0:1] * first_out + combine[:, 1:2] * second_out).astype(jnp.bfloat16)
    cot = cotangent.astype(jnp.float32)
    d_combine = jnp.stack(
        [jnp.sum(cot * first_out, axis=1), jnp.sum(cot * second_out, axis=1)], axis=1
    )
    first_cot = (combine[:, 0:1] * cot).astype(jnp.bfloat16)
    second_cot = (combine[:, 1:2] * cot).astype(jnp.bfloat16)
    send_cot = (dot_plain(pick_first, first_cot) + dot_plain(pick_second, second_cot)).astype(
        jnp.bfloat16
    )
    cot_rows = lax.all_to_all(
        send_cot.reshape(experts, capacity, width),
        "expert",
        split_axis=0,
        concat_axis=0,
        tiled=True,
    ).reshape(slot_total, width)
    group_cot = lax.all_gather(cot_rows, "dp", axis=0, tiled=True)
    d_hidden = dot_last(group_cot, local_down)
    d_gate, d_up = gate_grads(d_hidden, gate_pre, up_pre, sigmoid_gate)
    back_terms = dot_last(d_gate, local_gate) + dot_last(d_up, local_up)
    back_rows = lax.psum_scatter(
        back_terms.astype(jnp.bfloat16), "dp", scatter_dimension=0, tiled=True
    )
    grad_gate = group_total(group_rows, d_gate, groups)
    grad_up = group_total(group_rows, d_up, groups)
    grad_down = group_total(hidden, group_cot, groups)
    arrived = lax.all_to_all(
        back_rows.reshape(experts, capacity, width),
        "expert",
        split_axis=0,
        concat_axis=0,
        tiled=True,
    ).reshape(slot_total, width)
    d_tokens = dot_first(pick_both, arrived).astype(jnp.bfloat16)
    return (out, d_tokens, d_combine, grad_gate[None], grad_up[None], grad_down[None])


def solution(mesh):
    placed = (
        P(("dp", "expert"), None),
        P(("dp", "expert"), None),
        P(("dp", "expert"), None),
        P("expert", None, "dp"),
        P("expert", None, "dp"),
        P("expert", "dp", None),
        P(("dp", "expert"), None),
    )
    return jax.shard_map(
        on_device,
        mesh=mesh,
        in_specs=placed,
        out_specs=(
            P(("dp", "expert"), None),
            P(("dp", "expert"), None),
            P(("dp", "expert"), None),
            P("expert", None, "dp"),
            P("expert", None, "dp"),
            P("expert", "dp", None),
        ),
        check_vma=False,
    )
```

profile of v0, /device:TPU:0, one launch (start us, length us, event | category | flops | bytes accessed | tf_op | source)
XLA Modules:
  0.0 369.1 jit_solution(4682465402896897959)
XLA Ops:
  7.2 0.0 copy-start
  7.2 0.0 all-gather.3.cloned.1.call-start
  7.2 0.9 copy.21
  8.1 0.1 eq.60
  8.2 0.1 eq.56
  8.4 0.6 reduce-window.6
  9.0 0.2 slice_reduce_fusion
  9.2 0.1 fusion.37
  9.3 0.1 reduce_sum.66
  9.5 0.1 copy.23
  9.5 0.7 multiply_add_fusion
  10.3 1.4 convolution_convert_fusion.4
  11.7 19.7 %all_to_all.20 = bf16[8,40,1536]{2,1,0:T(8,128)(2,1)} all-to-all(bf16[8,40,1536]{2,1,0:T(8,128)(2,1)S(1)} %bitcast.77), channel_id=1, replica_groups=mesh['dp'=4,'expert'=8] {'expert'}, dimensions={0} | all-to-all | bytes 1966080 | tf_op jit(solution)/shard_map/all_to_all | solution.py:55
  31.4 0.0 all-gather.3.cloned.1.call-update
  31.5 0.0 all-gather.5.cloned.1.call-start
  31.5 0.5 fusion.17
  32.1 0.5 fusion.1
  32.6 17.7 %all_to_all.21 = bf16[8,40,1536]{2,1,0:T(8,128)(2,1)} all-to-all(bf16[8,40,1536]{2,1,0:T(8,128)(2,1)S(1)} %bitcast.76), channel_id=1, replica_groups=mesh['dp'=4,'expert'=8] {'expert'}, dimensions={0} | all-to-all | bytes 1966080 | tf_op jit(solution)/shard_map/all_to_all | solution.py:88
  50.3 0.0 all-gather.5.cloned.1.call-update
  50.3 0.0 reduce-scatter.3.cloned.1.call-start
  50.4 57.0 %all-gather.3.cloned.1.call-done = bf16[1280,1536]{1,0:T(8,128)(2,1)} async-done(((bf16[320,1536]{1,0:T(8,128)(2,1)}), bf16[1280,1536]{1,0:T(8,128)(2,1)}) %all-gather.3.cloned.1.call-update) | async-done | bytes 3932176 | tf_op jit(solution)/shard_map/all_gather | solution.py:61
  107.4 6.1 %fusion.6 = f32[1280,384]{1,0:T(8,128)} fusion(bf16[1280,1536]{1,0:T(8,128)(2,1)} %all-gather.3.cloned.1.call-done, bf16[1,1536,384]{2,1,0:T(8,128)(2,1)} %param.11), kind=kOutput, calls=%fused_computation.22 | convolution fusion | flops 1509949440 | bytes 7077888 | tf_op jit(solution)/shard_map/dot_general | solution.py:8
  113.5 3.5 fusion.10
  117.0 66.9 %all-gather.5.cloned.1.call-done = bf16[1280,1536]{1,0:T(8,128)(2,1)} async-done(((bf16[320,1536]{1,0:T(8,128)(2,1)}), bf16[1280,1536]{1,0:T(8,128)(2,1)}) %all-gather.5.cloned.1.call-update) | async-done | bytes 3932176 | tf_op jit(solution)/shard_map/all_gather | solution.py:95
  184.0 6.2 %multiply_convert_fusion = (bf16[1280,384]{1,0:T(8,128)(2,1)S(1)}, bf16[1280,384]{1,0:T(8,128)(2,1)S(1)}, bf16[1280,384]{1,0:T(8,128)(2,1)S(1)}) fusion(f32[1280,384]{1,0:T(8,128)} %fusion.10, f32[1280,384]{1,0:T(8,128)} %fusion.6, bf16[1280,1536]{1,0:T(8,128)(2,1)} %all-gather.5.cloned.1.call-done, bf16[1,384,1536]{2,1,0:T(8,128)(2,1)S(1)} %copy-done), kind=kOutput, calls=%fused_computation.10 | convolution fusion | flops 1517813760 | bytes 11993088 | tf_op jit(solution)/shard_map/dot_general | solution.py:12
  190.2 0.0 copy-start.5
  190.2 0.9 copy-done.5
  191.1 4.1 %convolution_convert_fusion = bf16[1280,1536]{1,0:T(8,128)(2,1)} fusion(bf16[1280,384]{1,0:T(8,128)(2,1)S(1)} %get-tuple-element.10, bf16[1,384,1536]{2,1,0:T(8,128)(2,1)S(1)} %copy-done), kind=kOutput, calls=%fused_computation.2 | convolution fusion | flops 1511915520 | bytes 6094848 | tf_op jit(solution)/shard_map/dot_general | solution.py:8
  195.2 0.0 reduce-scatter.3.cloned.1.call-update
  195.2 0.2 reduce-scatter.5.cloned.1.call-start
  195.5 3.6 fusion.8
  199.1 4.2 %fusion = bf16[1280,1536]{1,0:T(8,128)(2,1)} fusion(f32[1280,1536]{1,0:T(8,128)S(1)} %fusion.8, bf16[1280,384]{1,0:T(8,128)(2,1)S(1)} %get-tuple-element.8, bf16[1,1536,384]{2,1,0:T(8,128)(2,1)S(1)} %copy-done.7), kind=kOutput, calls=%fused_computation.1 | convolution fusion | flops 1513881600 | bytes 13959168 | tf_op jit(solution)/shard_map/dot_general | solution.py:12
  203.3 0.0 reduce-scatter.5.cloned.1.call-update
  203.3 63.2 %reduce-scatter.3.cloned.1.call-done = bf16[320,1536]{1,0:T(8,128)(2,1)} async-done(((bf16[1280,1536]{1,0:T(8,128)(2,1)}), bf16[320,1536]{1,0:T(8,128)(2,1)}) %reduce-scatter.3.cloned.1.call-update) | async-done | bytes 983056 | tf_op jit(solution)/shard_map/reduce_scatter | solution.py:66
  266.5 3.6 all-to-all-start.1
  270.2 7.3 %convolution_convert_fusion.1 = bf16[4,384,1536]{2,1,0:T(8,128)(2,1)} fusion(bf16[4,320,384]{2,1,0:T(8,128)(2,1)} %bitcast.79, bf16[4,320,1536]{2,1,0:T(8,128)(2,1)} %bitcast.69), kind=kOutput, calls=%fused_computation.3 | convolution fusion | flops 1512308736 | bytes 9633792 | tf_op jit(solution)/shard_map/gri,grj->gij/dot_general | solution.py:26
  277.5 4.8 %convolution_convert_fusion.3 = bf16[4,1536,384]{2,1,0:T(8,128)(2,1)} fusion(bf16[4,320,1536]{2,1,0:T(8,128)(2,1)S(1)} %bitcast.68, bf16[4,320,384]{2,1,0:T(8,128)(2,1)S(1)} %bitcast.72), kind=kOutput, calls=%fused_computation.5 | convolution fusion | flops 1512308736 | bytes 9633792 | tf_op jit(solution)/shard_map/gri,grj->gij/dot_general | solution.py:26
  282.3 4.5 %reduce_sum.71 = bf16[384,1536]{1,0:T(8,128)(2,1)} reduce(bf16[4,384,1536]{2,1,0:T(8,128)(2,1)} %convolution_convert_fusion.1, bf16[]{:T(256)} %constant.15.clone.1), dimensions={0}, to_apply=%region_9.10 | reduce | flops 1769472 | bytes 5898242 | tf_op jit(solution)/shard_map/reduce_sum | solution.py:28
  286.7 4.4 %reduce_sum.69 = bf16[1536,384]{1,0:T(8,128)(2,1)} reduce(bf16[4,1536,384]{2,1,0:T(8,128)(2,1)} %convolution_convert_fusion.3, bf16[]{:T(256)} %constant.15.clone.1), dimensions={0}, to_apply=%region_7.8 | reduce | flops 1769472 | bytes 5898242 | tf_op jit(solution)/shard_map/reduce_sum | solution.py:28
  291.1 50.7 %reduce-scatter.5.cloned.1.call-done = bf16[320,1536]{1,0:T(8,128)(2,1)} async-done(((bf16[1280,1536]{1,0:T(8,128)(2,1)}), bf16[320,1536]{1,0:T(8,128)(2,1)}) %reduce-scatter.5.cloned.1.call-update) | async-done | bytes 983056 | tf_op jit(solution)/shard_map/reduce_scatter | solution.py:99
  341.8 3.8 %all-to-all-start.3 = ((bf16[8,40,1536]{2,1,0:T(8,128)(2,1)}), bf16[8,40,1536]{2,1,0:T(8,128)(2,1)S(1)}, u32[]{:S(2)}, u32[]{:S(2)}) async-start(bf16[8,40,1536]{2,1,0:T(8,128)(2,1)} %bitcast.83), calls=%async_computation.5 | async-start | bytes 1966080 | tf_op jit(solution)/shard_map/all_to_all | solution.py:105
  345.6 7.6 %convolution_convert_fusion.2 = bf16[4,1536,384]{2,1,0:T(8,128)(2,1)} fusion(bf16[4,320,1536]{2,1,0:T(8,128)(2,1)} %bitcast.67, bf16[4,320,384]{2,1,0:T(8,128)(2,1)} %bitcast.78), kind=kOutput, calls=%fused_computation.4 | convolution fusion | flops 1512308736 | bytes 9633792 | tf_op jit(solution)/shard_map/gri,grj->gij/dot_general | solution.py:26
  353.1 4.4 %reduce_sum.70 = bf16[1536,384]{1,0:T(8,128)(2,1)} reduce(bf16[4,1536,384]{2,1,0:T(8,128)(2,1)} %convolution_convert_fusion.2, bf16[]{:T(256)} %constant.15.clone.1), dimensions={0}, to_apply=%region_8.9 | reduce | flops 1769472 | bytes 5898242 | tf_op jit(solution)/shard_map/reduce_sum | solution.py:28
  357.5 0.4 fusion.21
  357.9 1.9 fusion.14
  359.9 0.3 all-to-all-done.3
  360.1 1.2 convolution_convert_fusion.5
  361.3 1.3 pad_maximum_fusion
  (21 shorter events, 0.1 us)
Async XLA Ops:
  7.2 176.8 %copy-start = (bf16[1,384,1536]{2,1,0:T(8,128)(2,1)S(1)}, bf16[1,384,1536]{2,1,0:T(8,128)(2,1)}, u32[]{:S(2)}) copy-start(bf16[1,384,1536]{2,1,0:T(8,128)(2,1)} %param.12) | copy-start | bytes 3538948
  7.2 100.2 %all-gather.3.cloned.1.call-start = ((), (), s32[]{:S(2)}) async-start(), calls=%async_computation.6 | async-start | bytes 4915200 | tf_op jit(solution)/shard_map/all_gather | solution.py:61
  10.3 21.3 %copy-start.8 = (f32[128,2]{0,1:T(2,128)S(1)}, f32[128,2]{0,1:T(2,128)}, u32[]{:S(2)}) copy-start(f32[128,2]{0,1:T(2,128)} %param.9) | copy-start | bytes 3076
  10.3 21.3 %copy-start.4 = (bf16[128,1536]{1,0:T(8,128)(2,1)S(1)}, bf16[128,1536]{1,0:T(8,128)(2,1)}, u32[]{:S(2)}) copy-start(bf16[128,1536]{1,0:T(8,128)(2,1)} %param.13) | copy-start | bytes 1179652
  31.5 152.5 %all-gather.5.cloned.1.call-start = ((), (), s32[]{:S(2)}) async-start(), calls=%async_computation.8 | async-start | bytes 4915200 | tf_op jit(solution)/shard_map/all_gather | solution.py:95
  50.3 63.2 %copy-start.6 = (bf16[1,1536,384]{2,1,0:T(8,128)(2,1)S(1)}, bf16[1,1536,384]{2,1,0:T(8,128)(2,1)}, u32[]{:S(2)}) copy-start(bf16[1,1536,384]{2,1,0:T(8,128)(2,1)} %param.10) | copy-start | bytes 3538948
  50.3 216.2 %reduce-scatter.3.cloned.1.call-start = ((), (), s32[]{:S(2)}) async-start(), calls=%async_computation.7 | async-start | bytes 4915200 | tf_op jit(solution)/shard_map/reduce_scatter | solution.py:66
  107.4 6.1 %copy-start.1 = (bf16[1280,1536]{1,0:T(8,128)(2,1)S(1)}, bf16[1280,1536]{1,0:T(8,128)(2,1)}, u32[]{:S(2)}) copy-start(bf16[1280,1536]{1,0:T(8,128)(2,1)} %all-gather.3.cloned.1.call-done) | copy-start | bytes 11796484
  190.2 0.9 copy-start.5
  190.2 8.9 %copy-start.3 = (bf16[1280,384]{1,0:T(8,128)(2,1)}, bf16[1280,384]{1,0:T(8,128)(2,1)S(1)}, u32[]{:S(2)}) copy-start(bf16[1280,384]{1,0:T(8,128)(2,1)S(1)} %get-tuple-element.8) | copy-start | bytes 2949124
  195.2 146.6 %reduce-scatter.5.cloned.1.call-start = ((), (), s32[]{:S(2)}) async-start(), calls=%async_computation.9 | async-start | bytes 4915200 | tf_op jit(solution)/shard_map/reduce_scatter | solution.py:99
  195.5 3.6 copy-start.7
  266.5 75.3 %all-to-all-start.1 = ((bf16[8,40,1536]{2,1,0:T(8,128)(2,1)}), bf16[8,40,1536]{2,1,0:T(8,128)(2,1)S(1)}, u32[]{:S(2)}, u32[]{:S(2)}) async-start(bf16[8,40,1536]{2,1,0:T(8,128)(2,1)} %bitcast.84), calls=%async_computation.2 | async-start | bytes 1966080 | tf_op jit(solution)/shard_map/all_to_all | solution.py:69
  270.2 7.3 %copy-start.2 = (bf16[1280,1536]{1,0:T(8,128)(2,1)S(1)}, bf16[1280,1536]{1,0:T(8,128)(2,1)}, u32[]{:S(2)}) copy-start(bf16[1280,1536]{1,0:T(8,128)(2,1)} %all-gather.3.cloned.1.call-done) | copy-start | bytes 11796484
  341.8 18.3 %all-to-all-start.3 = ((bf16[8,40,1536]{2,1,0:T(8,128)(2,1)}), bf16[8,40,1536]{2,1,0:T(8,128)(2,1)S(1)}, u32[]{:S(2)}, u32[]{:S(2)}) async-start(bf16[8,40,1536]{2,1,0:T(8,128)(2,1)} %bitcast.83), calls=%async_computation.5 | async-start | bytes 1966080 | tf_op jit(solution)/shard_map/all_to_all | solution.py:105
Sparse Core Ops, SparseCore 0:
  31.6 75.7 all-gather.2
  109.0 74.9 all-gather.4
  195.3 71.1 reduce-scatter.2
  268.7 73.0 reduce-scatter.4
where the time goes:
time: 370 us; the launch traced here: 369 us
  waiting for transfers between devices  238 us (64%)
  matrix products  53.3 us (14%)
  blocking collectives  37.5 us (10%)
  other arithmetic  15.9 us (4%)
  between operations  13.9 us (4%)
  starting transfers between devices  7.77 us (2%)
    all_gather x1, waiting for transfers between devices, on_device(): group_cot = lax.all_gather(cot_rows, 'dp', axis=0, tiled=True)  66.9 us
    reduce_scatter x1, waiting for transfers between devices, on_device(): lax.psum_scatter(dot_plain(hidden, local_down).astype(jnp.bfloat16), 'dp'...  63.2 us
    all_gather x1, waiting for transfers between devices, on_device(): group_rows = lax.all_gather(token_rows, 'dp', axis=0, tiled=True)  57 us
    reduce_scatter x1, waiting for transfers between devices, on_device(): lax.psum_scatter(back_terms.astype(jnp.bfloat16), 'dp', scatter_dimension...  50.7 us
    all_to_all x1, blocking collectives, on_device(): lax.all_to_all(send_rows, 'expert', split_axis=0, concat_axis=0, tiled=True)  19.7 us
    dot_general x3, matrix products, group_total(): jnp.einsum('gri,grj->gij', left_groups, right_groups, preferred_element_t...  19.7 us
    all_to_all x1, blocking collectives, on_device(): lax.all_to_all(send_cot.reshape(experts, capacity, width), 'expert', spli...  17.7 us
    dot_general x6, matrix products, dot_plain(): return jnp.dot(left, right, preferred_element_type=jnp.float32)  16.1 us
  transfers between devices with their start and end apart: 6, of which 5 were waited for; matrix products, arithmetic and copies ran while one was open for 15% of the time, Pallas kernels for 0%

commit v1 on v0

--- a/solution.py
+++ b/solution.py
@@ -1,7 +1,371 @@
+import functools
+
 import jax
 import jax.numpy as jnp
 from jax import lax
+from jax.experimental import pallas as pl
+from jax.experimental.pallas import tpu as pltpu
 from jax.sharding import PartitionSpec as P
+
+MESH = pl.DeviceIdType.MESH
+
+
+def greet(groups, experts, d, e):
+    barrier = pltpu.get_barrier_semaphore()
+    for k in range(1, experts):
+        pl.semaphore_signal(
+            barrier, inc=1, device_id={"expert": lax.rem(e + k, experts)}, device_id_type=MESH
+        )
+
+    @pl.when(d > 0)
+    def _():
+        pl.semaphore_signal(barrier, inc=1, device_id={"dp": d - 1}, device_id_type=MESH)
+
+    @pl.when(d < groups - 1)
+    def _():
+        pl.semaphore_signal(barrier, inc=1, device_id={"dp": d + 1}, device_id_type=MESH)
+
+    beside = (d > 0).astype(jnp.int32) + (d < groups - 1).astype(jnp.int32)
+    pl.semaphore_wait(barrier, experts - 1 + beside)
+
+
+def picks(meta, expert, capacity):
+    count = meta.shape[1]
+    rows = lax.broadcasted_iota(jnp.int32, (capacity, count), 0) + expert * capacity
+    rows = rows.astype(jnp.float32)
+    return rows == meta[0:1, :], rows == meta[1:2, :]
+
+
+def dispatch_kernel(
+    groups, experts, capacity, tok_ref, cot_ref, meta_ref, tok_all, cot_all, cot_group, meta_all,
+    landed, meta_in, staged, line_send, line_recv, plane_send, plane_recv, local_sem, keep_sem,
+):
+    d = lax.axis_index("dp")
+    e = lax.axis_index("expert")
+    greet(groups, experts, d, e)
+    own = (tok_ref, cot_ref, meta_ref)
+    full = (tok_all, cot_all)
+
+    def line_copy(a, s, way, hop, first):
+        there = meta_in.at[s] if a == 2 else landed.at[a, s]
+        return pltpu.make_async_remote_copy(
+            src_ref=own[a] if first else there,
+            dst_ref=there,
+            send_sem=line_send.at[a, way, hop],
+            recv_sem=line_recv.at[a, way, hop],
+            device_id={"dp": d + 1 - 2 * way},
+            device_id_type=MESH,
+        )
+
+    def plane_copy(a, s, k):
+        other = lax.rem(e + k, experts)
+        return pltpu.make_async_remote_copy(
+            src_ref=staged.at[a, s, other],
+            dst_ref=full[a].at[s, e],
+            send_sem=plane_send.at[a, s, k],
+            recv_sem=plane_recv.at[a, s, k],
+            device_id={"expert": other},
+            device_id_type=MESH,
+        )
+
+    def local_copy(a, s):
+        return pltpu.make_async_copy(staged.at[a, s, e], full[a].at[s, e], local_sem.at[a, s])
+
+    def keep_copy(s):
+        return pltpu.make_async_copy(landed.at[1, s], cot_group.at[s], keep_sem.at[s])
+
+    def process(a, s, source, meta_view):
+        def rows_of(other):
+            meta = meta_view[...]
+            first, second = picks(meta, other, capacity)
+            onehot = (first | second).astype(jnp.bfloat16)
+            rows = jnp.dot(onehot, source[...], preferred_element_type=jnp.float32)
+            if a == 1:
+                weight = jnp.sum(
+                    jnp.where(first, meta[2:3, :], 0.0) + jnp.where(second, meta[3:4, :], 0.0),
+                    axis=1,
+                    keepdims=True,
+                )
+                rows = rows * weight
+            staged[a, s, other] = rows.astype(jnp.bfloat16)
+
+        def step(k, carry):
+            rows_of(lax.rem(e + k, experts))
+            plane_copy(a, s, k).start()
+            return carry
+
+        lax.fori_loop(1, experts, step, 0)
+        rows_of(e)
+        local_copy(a, s).start()
+
+    has_way = (d < groups - 1, d > 0)
+    for a in (2, 0, 1):
+        for way in (0, 1):
+
+            @pl.when(has_way[way])
+            def _(a=a, way=way):
+                line_copy(a, d, way, 1, True).start()
+
+    landed[1, d] = cot_ref[...]
+    meta_in[d] = meta_ref[...]
+    keep_copy(d).start()
+    process(0, d, tok_ref, meta_ref)
+    process(1, d, cot_ref, meta_ref)
+    for hop in range(1, groups):
+        for way in (0, 1):
+            s = d - hop + 2 * hop * way
+            came = (d - hop >= 0) if way == 0 else (d + hop < groups)
+
+            @pl.when(came)
+            def _(s=s, way=way, hop=hop):
+                for a in (2, 0, 1):
+                    line_copy(a, s, way, hop, False).wait_recv()
+                    if hop < groups - 1:
+
+                        @pl.when(has_way[way])
+                        def _():
+                            line_copy(a, s, way, hop + 1, False).start()
+
+                    if a < 2:
+                        process(a, s, landed.at[a, s], meta_in.at[s])
+                keep_copy(s).start()
+
+    for way in (0, 1):
+
+        @pl.when(has_way[way])
+        def _(way=way):
+            for a in range(3):
+                line_copy(a, d, way, 1, True).wait_send()
+
+        for hop in range(1, groups - 1):
+            s = d - hop + 2 * hop * way
+            came = (d - hop >= 0) if way == 0 else (d + hop < groups)
+
+            @pl.when(came & has_way[way])
+            def _(way=way, hop=hop, s=s):
+                for a in range(3):
+                    line_copy(a, s, way, hop + 1, False).wait_send()
+
+    def drain(s, carry):
+        keep_copy(s).wait()
+        for a in (0, 1):
+            local_copy(a, s).wait()
+
+            def one(k, inner, a=a):
+                plane_copy(a, s, k).wait()
+                return inner
+
+            lax.fori_loop(1, experts, one, 0)
+        return carry
+
+    lax.fori_loop(0, groups, drain, 0)
+    meta_all[...] = meta_in[...]
+
+
+def dispatch(groups, experts, capacity, tokens, cotangent, meta):
+    count, width = tokens.shape
+    table = jax.ShapeDtypeStruct((groups, experts, capacity, width), tokens.dtype)
+    anywhere = pl.BlockSpec(memory_space=pl.ANY)
+    vmem = pl.BlockSpec(memory_space=pltpu.VMEM)
+    dma = pltpu.SemaphoreType.DMA
+    return pl.pallas_call(
+        functools.partial(dispatch_kernel, groups, experts, capacity),
+        out_shape=(
+            table,
+            table,
+            jax.ShapeDtypeStruct((groups, count, width), tokens.dtype),
+            jax.ShapeDtypeStruct((groups,) + meta.shape, meta.dtype),
+        ),
+        in_specs=[vmem, vmem, vmem],
+        out_specs=(anywhere, anywhere, anywhere, vmem),
+        scratch_shapes=[
+            pltpu.VMEM((2, groups, count, width), tokens.dtype),
+            pltpu.VMEM((groups,) + meta.shape, meta.dtype),
+            pltpu.VMEM((2, groups, experts, capacity, width), tokens.dtype),
+            dma((3, 2, groups)),
+            dma((3, 2, groups)),
+            dma((2, groups, experts)),
+            dma((2, groups, experts)),
+            dma((2, groups)),
+            dma((groups,)),
+        ],
+        compiler_params=pltpu.CompilerParams(
+            collective_id=0, has_side_effects=True, vmem_limit_bytes=56 << 20
+        ),
+        name="dispatch",
+    )(tokens, cotangent, meta)
+
+
+def return_kernel(
+    groups, experts, capacity, out_rows, back_rows, cot_group, meta_ref, out_ref, back_ref, dc_ref,
+    landed, sums, dc_sums, line_in, dc_in, plane_send, plane_recv, local_sem,
+    line_send, line_recv,
+):
+    d = lax.axis_index("dp")
+    e = lax.axis_index("expert")
+    greet(groups, experts, d, e)
+    parts = (out_rows, back_rows)
+    count = cot_group.shape[1]
+    width = cot_group.shape[2]
+
+    def target(t):
+        low = d < groups - d - 1
+        m = jnp.where(low, d, groups - 1 - d)
+        j = jnp.where(t < groups - 1 - m, groups - 1 - t, t - (groups - 1 - m))
+        j = jnp.where(t == groups - 1, m, j)
+        return jnp.where(low, j, groups - 1 - j)
+
+    def plane_copy(a, t, k):
+        other = lax.rem(e + k, experts)
+        return pltpu.make_async_remote_copy(
+            src_ref=parts[a].at[target(t), other],
+            dst_ref=landed.at[a, t, e],
+            send_sem=plane_send.at[a, t, k],
+            recv_sem=plane_recv.at[a, t, k],
+            device_id={"expert": other},
+            device_id_type=MESH,
+        )
+
+    def local_copy(a, t):
+        return pltpu.make_async_copy(
+            parts[a].at[target(t), e], landed.at[a, t, e], local_sem.at[a, t]
+        )
+
+    def line_copy(a, j, way):
+        return pltpu.make_async_remote_copy(
+            src_ref=dc_sums.at[j] if a == 2 else sums.at[a, j],
+            dst_ref=dc_in.at[way, j] if a == 2 else line_in.at[a, way, j],
+            send_sem=line_send.at[a, way, j],
+            recv_sem=line_recv.at[a, way, j],
+            device_id={"dp": d + 1 - 2 * way},
+            device_id_type=MESH,
+        )
+
+    for t in range(groups):
+        for a in (0, 1):
+
+            def begin(k, carry, a=a, t=t):
+                plane_copy(a, t, k).start()
+                return carry
+
+            lax.fori_loop(1, experts, begin, 0)
+            local_copy(a, t).start()
+
+    def gathered(a, t, meta, which):
+        total = None
+        for other in range(experts):
+            first, second = picks(meta, other, capacity)
+            mask = (first, second, first | second)[which].astype(jnp.bfloat16)
+            term = lax.dot_general(
+                mask,
+                landed[a, t, other],
+                (((0,), (0,)), ((), ())),
+                preferred_element_type=jnp.float32,
+            )
+            total = term if total is None else total + term
+        return total
+
+    for t in range(groups):
+        j = target(t)
+        meta = meta_ref[j]
+        for a in (0, 1):
+            local_copy(a, t).wait()
+
+            def arrive(k, carry, a=a, t=t):
+                plane_copy(a, t, k).wait()
+                return carry
+
+            lax.fori_loop(1, experts, arrive, 0)
+            if a == 0:
+                lane = lax.broadcasted_iota(jnp.int32, (count, 128), 1)
+                cot = cot_group[j].astype(jnp.float32)
+                weights = jnp.transpose(meta)
+                mixed = None
+                dots = jnp.zeros((count, 128), jnp.float32)
+                for which in (0, 1):
+                    rows = gathered(0, t, meta, which)
+                    dot = jnp.sum(cot * rows, axis=1, keepdims=True)
+                    dots = jnp.where(lane == which, dot, dots)
+                    term = weights[:, 2 + which : 3 + which] * rows
+                    mixed = term if mixed is None else mixed + term
+                dc_sums[j] = dots
+                sums[0, j] = mixed.astype(jnp.bfloat16)
+            else:
+                sums[1, j] = gathered(1, t, meta, 2).astype(jnp.bfloat16)
+            for b in (0, 2) if a == 0 else (1,):
+
+                def add(way, b=b, j=j):
+                    line_copy(b, j, way).wait_recv()
+                    if b == 2:
+                        dc_sums[j] = dc_sums[j] + dc_in[way, j]
+                    else:
+                        sums[b, j] = (
+                            sums[b, j].astype(jnp.float32) + line_in[b, way, j].astype(jnp.float32)
+                        ).astype(jnp.bfloat16)
+
+                @pl.when((j >= d) & (d > 0))
+                def _(add=add):
+                    add(0)
+
+                @pl.when((j <= d) & (d < groups - 1))
+                def _(add=add):
+                    add(1)
+
+                @pl.when(j > d)
+                def _(b=b, j=j):
+                    line_copy(b, j, 0).start()
+
+                @pl.when(j < d)
+                def _(b=b, j=j):
+                    line_copy(b, j, 1).start()
+
+    out_ref[...] = sums[0, d]
+    back_ref[...] = sums[1, d]
+    dc_ref[...] = dc_sums[d]
+    for j in range(groups):
+        for b in range(3):
+
+            @pl.when(j > d)
+            def _(b=b, j=j):
+                line_copy(b, j, 0).wait_send()
+
+            @pl.when(j < d)
+            def _(b=b, j=j):
+                line_copy(b, j, 1).wait_send()
+
+
+def give_back(groups, experts, capacity, out_rows, back_rows, cot_group, meta_all):
+    count, width = cot_group.shape[1:]
+    anywhere = pl.BlockSpec(memory_space=pl.ANY)
+    vmem = pl.BlockSpec(memory_space=pltpu.VMEM)
+    dma = pltpu.SemaphoreType.DMA
+    kind = cot_group.dtype
+    return pl.pallas_call(
+        functools.partial(return_kernel, groups, experts, capacity),
+        out_shape=(
+            jax.ShapeDtypeStruct((count, width), kind),
+            jax.ShapeDtypeStruct((count, width), kind),
+            jax.ShapeDtypeStruct((count, 128), jnp.float32),
+        ),
+        in_specs=[anywhere, anywhere, vmem, vmem],
+        out_specs=(vmem, vmem, vmem),
+        scratch_shapes=[
+            pltpu.VMEM((2, groups, experts, capacity, width), kind),
+            pltpu.VMEM((2, groups, count, width), kind),
+            pltpu.VMEM((groups, count, 128), jnp.float32),
+            pltpu.VMEM((2, 2, groups, count, width), kind),
+            pltpu.VMEM((2, groups, count, 128), jnp.float32),
+            dma((2, groups, experts)),
+            dma((2, groups, experts)),
+            dma((2, groups)),
+            dma((3, 2, groups)),
+            dma((3, 2, groups)),
+        ],
+        compiler_params=pltpu.CompilerParams(
+            collective_id=1, has_side_effects=True, vmem_limit_bytes=56 << 20
+        ),
+        name="give_back",
+    )(out_rows, back_rows, cot_group, meta_all)
 
 
 def dot_plain(left, right):
@@ -36,7 +400,7 @@
     return (d_gate, d_up)
 
 
-def on_device(tokens, routes, combine, w_gate, w_up, w_down, cotangent):
+def plain_device(tokens, routes, combine, w_gate, w_up, w_down, cotangent):
     experts = lax.axis_size("expert")
     groups = lax.axis_size("dp")
     count = tokens.shape[0]
@@ -113,6 +477,47 @@
     return (out, d_tokens, d_combine, grad_gate[None], grad_up[None], grad_down[None])
 
 
+def on_device(tokens, routes, combine, w_gate, w_up, w_down, cotangent):
+    experts = lax.axis_size("expert")
+    groups = lax.axis_size("dp")
+    count, width = tokens.shape
+    capacity = 10 * count // (4 * experts)
+    if capacity % 8 or count % 128 or width % 128 or groups < 2:
+        return plain_device(tokens, routes, combine, w_gate, w_up, w_down, cotangent)
+    flat = routes.reshape(-1)
+    onehot = (flat[:, None] == jnp.arange(experts, dtype=jnp.int32)[None, :]).astype(jnp.int32)
+    before = jnp.cumsum(onehot, axis=0) - onehot
+    target_row = (flat * capacity + jnp.sum(before * onehot, axis=1)).reshape(count, 2)
+    meta = jnp.concatenate(
+        [target_row.astype(jnp.float32).T, combine.T, jnp.zeros((4, count), jnp.float32)], axis=0
+    )
+    table = (groups, experts, capacity, width)
+    tok_all, cot_all, cot_group, meta_all = dispatch(
+        groups, experts, capacity, tokens, cotangent, meta
+    )
+    group_rows = tok_all.reshape(-1, width)
+    group_cot = cot_all.reshape(-1, width)
+    local_gate = w_gate[0]
+    local_up = w_up[0]
+    local_down = w_down[0]
+    gate_pre = dot_plain(group_rows, local_gate)
+    up_pre = dot_plain(group_rows, local_up)
+    sigmoid_gate = jax.nn.sigmoid(gate_pre)
+    hidden = (gate_pre * sigmoid_gate * up_pre).astype(jnp.bfloat16)
+    out_part = dot_plain(hidden, local_down).astype(jnp.bfloat16)
+    d_hidden = dot_last(group_cot, local_down)
+    d_gate, d_up = gate_grads(d_hidden, gate_pre, up_pre, sigmoid_gate)
+    back_part = (dot_last(d_gate, local_gate) + dot_last(d_up, local_up)).astype(jnp.bfloat16)
+    out, d_tokens, dots = give_back(
+        groups, experts, capacity, out_part.reshape(table), back_part.reshape(table),
+        cot_group, meta_all,
+    )
+    grad_gate = dot_first(group_rows, d_gate).astype(jnp.bfloat16)
+    grad_up = dot_first(group_rows, d_up).astype(jnp.bfloat16)
+    grad_down = dot_first(hidden, group_cot).astype(jnp.bfloat16)
+    return (out, d_tokens, dots[:, :2], grad_gate[None], grad_up[None], grad_down[None])
+
+
 def solution(mesh):
     placed = (
         P(("dp", "expert"), None),

time: 370 us -> 227 us (0.61)
  waiting for transfers between devices: 238 us -> 0 us
  Pallas kernels: 0 us -> 186 us
  blocking collectives: 37.5 us -> 0 us
  matrix products: 53.3 us -> 29.9 us
  other arithmetic: 15.9 us -> 2.77 us
  between operations: 13.9 us -> 0.79 us
  starting transfers between devices: 7.77 us -> 0 us
  local copies, waits for them, and re-layouts: 2.55 us -> 6.67 us
    pallas_call x0 -> x2, Pallas kernels: none -> 186 us  [the longest x1 93.4 us: give_back(): pl.pallas_call(functools.partial(return_kernel, groups, experts, capacity...]
    all_gather x2 -> x0, waiting for transfers between devices: 124 us -> none  [the longest x1 66.9 us: on_device(): group_cot = lax.all_gather(cot_rows, 'dp', axis=0, tiled=True)]
    reduce_scatter x2 -> x0, waiting for transfers between devices: 114 us -> none  [the longest x1 63.2 us: on_device(): lax.psum_scatter(dot_plain(hidden, local_down).astype(jnp.bfloat16), 'dp'...]
    all_to_all x2 -> x0, blocking collectives: 37.5 us -> none  [the longest x1 19.7 us: on_device(): lax.all_to_all(send_rows, 'expert', split_axis=0, concat_axis=0, tiled=True)]
    dot_general x3 -> x0, matrix products: 19.7 us -> none  [group_total(): jnp.einsum('gri,grj->gij', left_groups, right_groups, preferred_element_t...]
    reduce_sum x3 -> x0, other arithmetic: 13.2 us -> none  [group_total(): return jnp.sum(part, axis=0).astype(jnp.bfloat16)]
    all_to_all x2 -> x0, starting transfers between devices: 7.42 us -> none  [the longest x1 3.78 us: on_device(): lax.all_to_all(back_rows.reshape(experts, capacity, width), 'expert', spl...]
    dot_general x3, matrix products: 3.49 us -> 9.24 us  [dot_first(): lax.dot_general(left, right, (((0,), (0,)), ((), ())), preferred_element_...]
  transfers between devices with their start and end apart: 6 -> 0, of which waited for: 5 -> 0; matrix products, arithmetic and copies ran while one was open for 15% -> 0% of each run, Pallas kernels for 0% -> 0%
where the time goes in v1:
time: 227 us; the launch traced here: 226 us
  Pallas kernels  186 us (82%)
  matrix products  29.9 us (13%)
  local copies, waits for them, and re-layouts  6.67 us (3%)
  other arithmetic  2.77 us (1%)
    pallas_call x1, Pallas kernels, give_back(): pl.pallas_call(functools.partial(return_kernel, groups, experts, capacity...  93.4 us
    pallas_call x1, Pallas kernels, dispatch(): pl.pallas_call(functools.partial(dispatch_kernel, groups, experts, capaci...  92.6 us
    dot_general x3, matrix products, dot_plain(): return jnp.dot(left, right, preferred_element_type=jnp.float32)  11.1 us
    dot_general x3, matrix products, dot_last(): lax.dot_general(left, right, (((1,), (1,)), ((), ())), preferred_element_...  9.59 us
    dot_general x3, matrix products, dot_first(): lax.dot_general(left, right, (((0,), (0,)), ((), ())), preferred_element_...  9.24 us
    unnamed x14, local copies, waits for them, and re-layouts  5.9 us

profile of v1, /device:TPU:0, one launch (start us, length us, event | category | flops | bytes accessed | tf_op | source)
XLA Modules:
  0.0 226.2 jit_solution(16226696778576566319)
XLA Ops:
  0.6 0.0 copy-start
  0.7 0.1 pad.2.clone
  0.7 0.9 copy.14
  1.6 0.1 eq.29
  1.7 0.1 eq.25
  1.9 0.6 reduce-window.6
  2.5 0.2 slice_reduce_fusion
  2.7 0.1 fusion.15
  2.8 0.1 reduce_sum.12
  3.0 0.1 copy.16
  3.0 0.7 convert_bitcast_fusion
  3.7 1.3 maximum_maximum_fusion.meta_ref
  5.1 92.6 %dispatch.1 = (bf16[4,8,40,1536]{3,2,1,0:T(8,128)(2,1)}, bf16[4,8,40,1536]{3,2,1,0:T(8,128)(2,1)}, bf16[4,128,1536]{2,1,0:T(8,128)(2,1)}, f32[4,8,128]{2,1,0:T(8,128)}) custom-call(bf16[128,1536]{1,0:T(8,128)(2,1)} %tok_ref.1, bf16[128,1536]{1,0:T(8,128)(2,1)} %cot_ref.1, f32[8,128]{1,0:T(8,128)} %maximum_maximum_fusion.meta_ref), custom_call_target="tpu_custom_call" | custom-call | tf_op jit(solution)/shard_map/dispatch/pallas_call | solution.py:171
  97.7 0.0 copy-start.1
  97.7 0.0 copy-start.3
  97.7 4.8 %fusion.8 = f32[1280,384]{1,0:T(8,128)S(1)} fusion(bf16[1280,1536]{1,0:T(8,128)(2,1)} %bitcast.55, bf16[1,1536,384]{2,1,0:T(8,128)(2,1)} %param.11), kind=kOutput, calls=%fused_computation.17 | convolution fusion | flops 1509949440 | bytes 7077888 | tf_op jit(solution)/shard_map/dot_general | solution.py:372
  102.5 0.0 copy-done.1
  102.6 0.0 copy-done.3
  102.6 0.0 copy-start.4
  102.6 2.2 fusion.12
  104.8 0.0 copy-done
  104.8 0.0 copy-done.4
  104.8 2.9 %multiply_convert_fusion = (bf16[1280,384]{1,0:T(8,128)(2,1)S(1)}, bf16[1280,384]{1,0:T(8,128)(2,1)S(1)}, bf16[1280,384]{1,0:T(8,128)(2,1)S(1)}) fusion(f32[1280,384]{1,0:T(8,128)S(1)} %fusion.12, f32[1280,384]{1,0:T(8,128)S(1)} %fusion.8, bf16[1280,1536]{1,0:T(8,128)(2,1)S(1)} %bitcast.59, bf16[1,384,1536]{2,1,0:T(8,128)(2,1)S(1)} %copy-done), kind=kOutput, calls=%fused_computation.9 | convolution fusion | flops 1517813760 | bytes 11993088 | tf_op jit(solution)/shard_map/dot_general | solution.py:376
  107.7 2.7 %fusion.3 = bf16[1,384,1536]{2,1,0:T(8,128)(2,1)} fusion(bf16[1280,384]{1,0:T(8,128)(2,1)S(1)} %get-tuple-element.34, bf16[1280,1536]{1,0:T(8,128)(2,1)S(1)} %bitcast.60), kind=kOutput, calls=%fused_computation.8 | convolution fusion | flops 1510539264 | bytes 6094848 | tf_op jit(solution)/shard_map/dot_general | solution.py:382
  110.5 3.3 %fusion.2 = bf16[1,1536,384]{2,1,0:T(8,128)(2,1)} fusion(bf16[1280,1536]{1,0:T(8,128)(2,1)S(1)} %bitcast.57, bf16[1280,384]{1,0:T(8,128)(2,1)S(1)} %get-tuple-element.32), kind=kOutput, calls=%fused_computation.7 | convolution fusion | flops 1510539264 | bytes 6094848 | tf_op jit(solution)/shard_map/dot_general | solution.py:382
  113.7 3.3 %fusion.1 = bf16[1,1536,384]{2,1,0:T(8,128)(2,1)} fusion(bf16[1280,1536]{1,0:T(8,128)(2,1)S(1)} %bitcast.58, bf16[1280,384]{1,0:T(8,128)(2,1)S(1)} %get-tuple-element.33), kind=kOutput, calls=%fused_computation.6 | convolution fusion | flops 1510539264 | bytes 6094848 | tf_op jit(solution)/shard_map/dot_general | solution.py:382
  117.0 4.1 %convolution_convert_fusion = bf16[1280,1536]{1,0:T(8,128)(2,1)} fusion(bf16[1280,384]{1,0:T(8,128)(2,1)S(1)} %get-tuple-element.34, bf16[1,384,1536]{2,1,0:T(8,128)(2,1)S(1)} %copy-done), kind=kOutput, calls=%fused_computation.2 | convolution fusion | flops 1511915520 | bytes 6094848 | tf_op jit(solution)/shard_map/dot_general | solution.py:372
  121.1 0.0 copy-start.2
  121.1 2.5 %fusion.10 = f32[1280,1536]{1,0:T(8,128)S(1)} fusion(bf16[1280,384]{1,0:T(8,128)(2,1)S(1)} %get-tuple-element.33, bf16[1,1536,384]{2,1,0:T(8,128)(2,1)S(1)} %copy-done.1), kind=kOutput, calls=%fused_computation.19 | convolution fusion | flops 1509949440 | bytes 10027008 | tf_op jit(solution)/shard_map/dot_general | solution.py:376
  123.5 0.0 copy-done.2
  123.6 4.2 %fusion = bf16[1280,1536]{1,0:T(8,128)(2,1)} fusion(f32[1280,1536]{1,0:T(8,128)S(1)} %fusion.10, bf16[1280,384]{1,0:T(8,128)(2,1)S(1)} %get-tuple-element.32, bf16[1,1536,384]{2,1,0:T(8,128)(2,1)S(1)} %copy-done.2), kind=kOutput, calls=%fused_computation.1 | convolution fusion | flops 1513881600 | bytes 13959168 | tf_op jit(solution)/shard_map/dot_general | solution.py:376
  127.7 93.4 %give_back.1 = (bf16[128,1536]{1,0:T(8,128)(2,1)}, bf16[128,1536]{1,0:T(8,128)(2,1)}, f32[128,128]{1,0:T(8,128)}) custom-call(bf16[4,8,40,1536]{3,2,1,0:T(8,128)(2,1)} %bitcast.52, bf16[4,8,40,1536]{3,2,1,0:T(8,128)(2,1)} %bitcast.51, bf16[4,128,1536]{2,1,0:T(8,128)(2,1)} %get-tuple-element.15.cot_group, f32[4,8,128]{2,1,0:T(8,128)} %get-tuple-element.16.meta_ref), custom_call_target="tpu_custom_call" | custom-call | tf_op jit(solution)/shard_map/give_back/pallas_call | solution.py:343
  221.2 1.5 copy.17
  222.6 1.8 copy.20
  224.4 1.8 copy.21
  (4 shorter events, 0.0 us)
Async XLA Ops:
  0.6 104.1 %copy-start = (bf16[1,384,1536]{2,1,0:T(8,128)(2,1)S(1)}, bf16[1,384,1536]{2,1,0:T(8,128)(2,1)}, u32[]{:S(2)}) copy-start(bf16[1,384,1536]{2,1,0:T(8,128)(2,1)} %param.12) | copy-start | bytes 3538948
  97.7 4.8 %copy-start.1 = (bf16[1,1536,384]{2,1,0:T(8,128)(2,1)S(1)}, bf16[1,1536,384]{2,1,0:T(8,128)(2,1)}, u32[]{:S(2)}) copy-start(bf16[1,1536,384]{2,1,0:T(8,128)(2,1)} %param.10) | copy-start | bytes 3538948
  97.7 4.8 %copy-start.3 = (bf16[4,8,40,1536]{3,2,1,0:T(8,128)(2,1)S(1)}, bf16[4,8,40,1536]{3,2,1,0:T(8,128)(2,1)}, u32[]{:S(2)}) copy-start(bf16[4,8,40,1536]{3,2,1,0:T(8,128)(2,1)} %get-tuple-element.13) | copy-start | bytes 11796484
  102.6 2.2 copy-start.4
  121.1 2.5 %copy-start.2 = (bf16[1,1536,384]{2,1,0:T(8,128)(2,1)S(1)}, bf16[1,1536,384]{2,1,0:T(8,128)(2,1)}, u32[]{:S(2)}) copy-start(bf16[1,1536,384]{2,1,0:T(8,128)(2,1)} %param.11) | copy-start | bytes 3538948

commit v2 on v1

--- a/solution.py
+++ b/solution.py
@@ -29,6 +29,11 @@
     pl.semaphore_wait(barrier, experts - 1 + beside)
 
 
+def split(width):
+    half = width // 256 * 128
+    return (slice(0, half), slice(half, width))
+
+
 def picks(meta, expert, capacity):
     count = meta.shape[1]
     rows = lax.broadcasted_iota(jnp.int32, (capacity, count), 0) + expert * capacity
@@ -39,11 +44,14 @@
 def dispatch_kernel(
     groups, experts, capacity, tok_ref, cot_ref, meta_ref, tok_all, cot_all, cot_group, meta_all,
     landed, meta_in, staged, line_send, line_recv, plane_send, plane_recv, local_sem, keep_sem,
+    table_send, table_recv,
 ):
     d = lax.axis_index("dp")
     e = lax.axis_index("expert")
     greet(groups, experts, d, e)
     own = (tok_ref, cot_ref, meta_ref)
+    partner = d + 1 - 2 * lax.rem(d, 2)
+    halves = split(tok_ref.shape[1])
     full = (tok_all, cot_all)
 
     def line_copy(a, s, way, hop, first):
@@ -57,19 +65,42 @@
             device_id_type=MESH,
         )
 
-    def plane_copy(a, s, k):
+    def plane_copy(h, a, s, k):
         other = lax.rem(e + k, experts)
         return pltpu.make_async_remote_copy(
-            src_ref=staged.at[a, s, other],
-            dst_ref=full[a].at[s, e],
-            send_sem=plane_send.at[a, s, k],
-            recv_sem=plane_recv.at[a, s, k],
+            src_ref=staged.at[a, s, other, :, halves[h]],
+            dst_ref=full[a].at[s, e, :, halves[h]],
+            send_sem=plane_send.at[h, a, s, k],
+            recv_sem=plane_recv.at[h, a, s, k],
             device_id={"expert": other},
             device_id_type=MESH,
         )
 
-    def local_copy(a, s):
-        return pltpu.make_async_copy(staged.at[a, s, e], full[a].at[s, e], local_sem.at[a, s])
+    def local_copy(h, a, s):
+        return pltpu.make_async_copy(
+            staged.at[a, s, e, :, halves[h]], full[a].at[s, e, :, halves[h]], local_sem.at[h, a, s]
+        )
+
+    def table_copy(a, k):
+        source = lax.rem(e + experts - k, experts)
+        block = full[a].at[d, source, :, halves[0]]
+        return pltpu.make_async_remote_copy(
+            src_ref=staged.at[a, d, e, :, halves[0]] if isinstance(k, int) else block,
+            dst_ref=block,
+            send_sem=table_send.at[a, k],
+            recv_sem=table_recv.at[a, k],
+            device_id={"dp": partner},
+            device_id_type=MESH,
+        )
+
+    def hand_over(a):
+        def one(k, carry):
+            plane_copy(0, a, d, k).wait_recv()
+            table_copy(a, k).start()
+            return carry
+
+        table_copy(a, 0).start()
+        lax.fori_loop(1, experts, one, 0)
 
     def keep_copy(s):
         return pltpu.make_async_copy(landed.at[1, s], cot_group.at[s], keep_sem.at[s])
@@ -91,12 +122,21 @@
 
         def step(k, carry):
             rows_of(lax.rem(e + k, experts))
-            plane_copy(a, s, k).start()
+            plane_copy(1, a, s, k).start()
+
+            @pl.when(s != partner)
+            def _():
+                plane_copy(0, a, s, k).start()
+
             return carry
 
         lax.fori_loop(1, experts, step, 0)
         rows_of(e)
-        local_copy(a, s).start()
+        local_copy(1, a, s).start()
+
+        @pl.when(s != partner)
+        def _():
+            local_copy(0, a, s).start()
 
     has_way = (d < groups - 1, d > 0)
     for a in (2, 0, 1):
@@ -130,6 +170,12 @@
                         process(a, s, landed.at[a, s], meta_in.at[s])
                 keep_copy(s).start()
 
+        if hop < 3:
+            hand_over(hop - 1)
+
+    for a in range(min(groups - 1, 2), 2):
+        hand_over(a)
+
     for way in (0, 1):
 
         @pl.when(has_way[way])
@@ -149,16 +195,36 @@
     def drain(s, carry):
         keep_copy(s).wait()
         for a in (0, 1):
-            local_copy(a, s).wait()
+            local_copy(1, a, s).wait()
+
+            @pl.when(s != partner)
+            def _(a=a):
+                local_copy(0, a, s).wait()
 
             def one(k, inner, a=a):
-                plane_copy(a, s, k).wait()
+                plane_copy(1, a, s, k).wait()
+
+                @pl.when(s != partner)
+                def _():
+                    plane_copy(0, a, s, k).wait_send()
+
+                @pl.when((s != partner) & (s != d))
+                def _():
+                    plane_copy(0, a, s, k).wait_recv()
+
                 return inner
 
             lax.fori_loop(1, experts, one, 0)
         return carry
 
     lax.fori_loop(0, groups, drain, 0)
+
+    def tables(k, carry):
+        for a in (0, 1):
+            table_copy(a, k).wait()
+        return carry
+
+    lax.fori_loop(0, experts, tables, 0)
     meta_all[...] = meta_in[...]
 
 
@@ -184,10 +250,12 @@
             pltpu.VMEM((2, groups, experts, capacity, width), tokens.dtype),
             dma((3, 2, groups)),
             dma((3, 2, groups)),
-            dma((2, groups, experts)),
-            dma((2, groups, experts)),
-            dma((2, groups)),
+            dma((2, 2, groups, experts)),
+            dma((2, 2, groups, experts)),
+            dma((2, 2, groups)),
             dma((groups,)),
+            dma((2, experts)),
+            dma((2, experts)),
         ],
         compiler_params=pltpu.CompilerParams(
             collective_id=0, has_side_effects=True, vmem_limit_bytes=56 << 20
@@ -199,14 +267,15 @@
 def return_kernel(
     groups, experts, capacity, out_rows, back_rows, cot_group, meta_ref, out_ref, back_ref, dc_ref,
     landed, sums, dc_sums, line_in, dc_in, plane_send, plane_recv, local_sem,
-    line_send, line_recv,
+    line_send, line_recv, table_in, table_own, table_send, table_recv, table_sem,
 ):
     d = lax.axis_index("dp")
     e = lax.axis_index("expert")
     greet(groups, experts, d, e)
     parts = (out_rows, back_rows)
     count = cot_group.shape[1]
-    width = cot_group.shape[2]
+    halves = split(cot_group.shape[2])
+    partner = d + 1 - 2 * lax.rem(d, 2)
 
     def target(t):
         low = d < groups - d - 1
@@ -215,20 +284,56 @@
         j = jnp.where(t == groups - 1, m, j)
         return jnp.where(low, j, groups - 1 - j)
 
-    def plane_copy(a, t, k):
+    def rows_for(h, a, t, other):
+        if h == 0 and t == groups - 1:
+            return table_own.at[a, other]
+        return parts[a].at[target(t), other, :, halves[h]]
+
+    def plane_copy(h, a, t, k):
         other = lax.rem(e + k, experts)
         return pltpu.make_async_remote_copy(
-            src_ref=parts[a].at[target(t), other],
-            dst_ref=landed.at[a, t, e],
-            send_sem=plane_send.at[a, t, k],
-            recv_sem=plane_recv.at[a, t, k],
+            src_ref=rows_for(h, a, t, other),
+            dst_ref=landed.at[a, t, e, :, halves[h]],
+            send_sem=plane_send.at[h, a, t, k],
+            recv_sem=plane_recv.at[h, a, t, k],
             device_id={"expert": other},
             device_id_type=MESH,
         )
 
-    def local_copy(a, t):
+    def local_copy(h, a, t):
         return pltpu.make_async_copy(
-            parts[a].at[target(t), e], landed.at[a, t, e], local_sem.at[a, t]
+            rows_for(h, a, t, e), landed.at[a, t, e, :, halves[h]], local_sem.at[h, a, t]
+        )
+
+    def send_rows(h, a, t):
+        def begin(k, carry):
+            plane_copy(h, a, t, k).start()
+            return carry
+
+        lax.fori_loop(1, experts, begin, 0)
+        local_copy(h, a, t).start()
+
+    def await_rows(h, a, t):
+        def arrive(k, carry):
+            plane_copy(h, a, t, k).wait()
+            return carry
+
+        local_copy(h, a, t).wait()
+        lax.fori_loop(1, experts, arrive, 0)
+
+    def table_copy(a):
+        return pltpu.make_async_remote_copy(
+            src_ref=parts[a].at[partner, :, :, halves[0]],
+            dst_ref=table_in.at[a],
+            send_sem=table_send.at[a],
+            recv_sem=table_recv.at[a],
+            device_id={"dp": partner},
+            device_id_type=MESH,
+        )
+
+    def own_table(a):
+        return pltpu.make_async_copy(
+            parts[a].at[d, :, :, halves[0]], table_own.at[a], table_sem.at[a]
         )
 
     def line_copy(a, j, way):
@@ -241,57 +346,81 @@
             device_id_type=MESH,
         )
 
+    for a in (0, 1):
+        table_copy(a).start()
+        own_table(a).start()
     for t in range(groups):
         for a in (0, 1):
-
-            def begin(k, carry, a=a, t=t):
-                plane_copy(a, t, k).start()
-                return carry
-
-            lax.fori_loop(1, experts, begin, 0)
-            local_copy(a, t).start()
-
-    def gathered(a, t, meta, which):
+            if t < groups - 1:
+
+                @pl.when(target(t) != partner)
+                def _(a=a, t=t):
+                    send_rows(0, a, t)
+
+            send_rows(1, a, t)
+    for a in (0, 1):
+        own_table(a).wait()
+        table_copy(a).wait()
+
+        def join(k, carry, a=a):
+            mine, other = table_own[a, k], table_in[a, k]
+            table_own[a, k] = (mine.astype(jnp.float32) + other.astype(jnp.float32)).astype(
+                mine.dtype
+            )
+            return carry
+
+        lax.fori_loop(0, experts, join, 0)
+        send_rows(0, a, groups - 1)
+
+    def gathered(h, a, t, meta, which):
         total = None
         for other in range(experts):
             first, second = picks(meta, other, capacity)
             mask = (first, second, first | second)[which].astype(jnp.bfloat16)
             term = lax.dot_general(
                 mask,
-                landed[a, t, other],
+                landed[a, t, other, :, halves[h]],
                 (((0,), (0,)), ((), ())),
                 preferred_element_type=jnp.float32,
             )
             total = term if total is None else total + term
         return total
 
+    def gather_half(h, a, t, j):
+        meta = meta_ref[j]
+        if a == 1:
+            sums[1, j, :, halves[h]] = gathered(h, 1, t, meta, 2).astype(jnp.bfloat16)
+            return
+        lane = lax.broadcasted_iota(jnp.int32, (count, 128), 1)
+        cot = cot_group[j, :, halves[h]].astype(jnp.float32)
+        weights = jnp.transpose(meta)
+        mixed = None
+        dots = jnp.zeros((count, 128), jnp.float32)
+        for which in (0, 1):
+            rows = gathered(h, 0, t, meta, which)
+            dot = jnp.sum(cot * rows, axis=1, keepdims=True)
+            dots = jnp.where(lane == which, dot, dots)
+            term = weights[:, 2 + which : 3 + which] * rows
+            mixed = term if mixed is None else mixed + term
+        dc_sums[j] = dc_sums[j] + dots
+        sums[0, j, :, halves[h]] = mixed.astype(jnp.bfloat16)
+
+    dc_sums[...] = jnp.zeros_like(dc_sums)
     for t in range(groups):
         j = target(t)
-        meta = meta_ref[j]
         for a in (0, 1):
-            local_copy(a, t).wait()
-
-            def arrive(k, carry, a=a, t=t):
-                plane_copy(a, t, k).wait()
-                return carry
-
-            lax.fori_loop(1, experts, arrive, 0)
-            if a == 0:
-                lane = lax.broadcasted_iota(jnp.int32, (count, 128), 1)
-                cot = cot_group[j].astype(jnp.float32)
-                weights = jnp.transpose(meta)
-                mixed = None
-                dots = jnp.zeros((count, 128), jnp.float32)
-                for which in (0, 1):
-                    rows = gathered(0, t, meta, which)
-                    dot = jnp.sum(cot * rows, axis=1, keepdims=True)
-                    dots = jnp.where(lane == which, dot, dots)
-                    term = weights[:, 2 + which : 3 + which] * rows
-                    mixed = term if mixed is None else mixed + term
-                dc_sums[j] = dots
-                sums[0, j] = mixed.astype(jnp.bfloat16)
-            else:
-                sums[1, j] = gathered(1, t, meta, 2).astype(jnp.bfloat16)
+
+            @pl.when(j == partner)
+            def _(a=a, j=j):
+                sums[a, j, :, halves[0]] = jnp.zeros((count, halves[0].stop), sums.dtype)
+
+            @pl.when(j != partner)
+            def _(a=a, t=t, j=j):
+                await_rows(0, a, t)
+                gather_half(0, a, t, j)
+
+            await_rows(1, a, t)
+            gather_half(1, a, t, j)
             for b in (0, 2) if a == 0 else (1,):
 
                 def add(way, b=b, j=j):
@@ -355,11 +484,16 @@
             pltpu.VMEM((groups, count, 128), jnp.float32),
             pltpu.VMEM((2, 2, groups, count, width), kind),
             pltpu.VMEM((2, groups, count, 128), jnp.float32),
-            dma((2, groups, experts)),
-            dma((2, groups, experts)),
-            dma((2, groups)),
+            dma((2, 2, groups, experts)),
+            dma((2, 2, groups, experts)),
+            dma((2, 2, groups)),
             dma((3, 2, groups)),
             dma((3, 2, groups)),
+            pltpu.VMEM((2, experts, capacity, split(width)[0].stop), kind),
+            pltpu.VMEM((2, experts, capacity, split(width)[0].stop), kind),
+            dma((2,)),
+            dma((2,)),
+            dma((2,)),
         ],
         compiler_params=pltpu.CompilerParams(
             collective_id=1, has_side_effects=True, vmem_limit_bytes=56 << 20
@@ -482,7 +616,7 @@
     groups = lax.axis_size("dp")
     count, width = tokens.shape
     capacity = 10 * count // (4 * experts)
-    if capacity % 8 or count % 128 or width % 128 or groups < 2:
+    if capacity % 8 or count % 128 or width % 128 or width < 256 or groups % 2:
         return plain_device(tokens, routes, combine, w_gate, w_up, w_down, cotangent)
     flat = routes.reshape(-1)
     onehot = (flat[:, None] == jnp.arange(experts, dtype=jnp.int32)[None, :]).astype(jnp.int32)

time: 227 us -> 220 us (0.969)
  Pallas kernels: 186 us -> 180 us
    pallas_call x1, Pallas kernels: 92.6 us -> 87.7 us  [dispatch(): pl.pallas_call(functools.partial(dispatch_kernel, groups, experts, capaci...]
where the time goes in v2:
time: 220 us
  Pallas kernels  180 us (82%)
  matrix products  29.9 us (14%)
  local copies, waits for them, and re-layouts  6.67 us (3%)
  other arithmetic  2.77 us (1%)
    pallas_call x1, Pallas kernels, give_back(): pl.pallas_call(functools.partial(return_kernel, groups, experts, capacity...  92.2 us
    pallas_call x1, Pallas kernels, dispatch(): pl.pallas_call(functools.partial(dispatch_kernel, groups, experts, capaci...  87.7 us
    dot_general x3, matrix products, dot_plain(): return jnp.dot(left, right, preferred_element_type=jnp.float32)  11.3 us
    dot_general x3, matrix products, dot_last(): lax.dot_general(left, right, (((1,), (1,)), ((), ())), preferred_element_...  9.35 us
    dot_general x3, matrix products, dot_first(): lax.dot_general(left, right, (((0,), (0,)), ((), ())), preferred_element_...  9.24 us
    unnamed x14, local copies, waits for them, and re-layouts  5.9 us

profile of v2, /device:TPU:0, one launch (start us, length us, event | category | flops | bytes accessed | tf_op | source)
XLA Modules:
  0.0 220.1 jit_solution(2700638428916380477)
XLA Ops:
  0.6 0.0 copy-start
  0.7 0.1 pad.2.clone
  0.7 0.9 copy.14
  1.6 0.1 eq.29
  1.7 0.1 eq.25
  1.9 0.6 reduce-window.6
  2.5 0.2 slice_reduce_fusion
  2.7 0.1 fusion.15
  2.8 0.1 reduce_sum.12
  3.0 0.1 copy.16
  3.0 0.7 convert_bitcast_fusion
  3.7 1.3 maximum_maximum_fusion.meta_ref
  5.1 87.7 %dispatch.1 = (bf16[4,8,40,1536]{3,2,1,0:T(8,128)(2,1)}, bf16[4,8,40,1536]{3,2,1,0:T(8,128)(2,1)}, bf16[4,128,1536]{2,1,0:T(8,128)(2,1)}, f32[4,8,128]{2,1,0:T(8,128)}) custom-call(bf16[128,1536]{1,0:T(8,128)(2,1)} %tok_ref.1, bf16[128,1536]{1,0:T(8,128)(2,1)} %cot_ref.1, f32[8,128]{1,0:T(8,128)} %maximum_maximum_fusion.meta_ref), custom_call_target="tpu_custom_call" | custom-call | tf_op jit(solution)/shard_map/dispatch/pallas_call | solution.py:237
  92.8 0.0 copy-start.1
  92.9 0.0 copy-start.3
  92.9 4.8 %fusion.8 = f32[1280,384]{1,0:T(8,128)S(1)} fusion(bf16[1280,1536]{1,0:T(8,128)(2,1)} %bitcast.55, bf16[1,1536,384]{2,1,0:T(8,128)(2,1)} %param.11), kind=kOutput, calls=%fused_computation.17 | convolution fusion | flops 1509949440 | bytes 7077888 | tf_op jit(solution)/shard_map/dot_general | solution.py:506
  97.7 0.0 copy-done.1
  97.7 0.0 copy-done.3
  97.7 0.0 copy-start.4
  97.7 2.2 fusion.12
  99.9 0.0 copy-done
  99.9 0.0 copy-done.4
  99.9 2.9 %multiply_convert_fusion = (bf16[1280,384]{1,0:T(8,128)(2,1)S(1)}, bf16[1280,384]{1,0:T(8,128)(2,1)S(1)}, bf16[1280,384]{1,0:T(8,128)(2,1)S(1)}) fusion(f32[1280,384]{1,0:T(8,128)S(1)} %fusion.12, f32[1280,384]{1,0:T(8,128)S(1)} %fusion.8, bf16[1280,1536]{1,0:T(8,128)(2,1)S(1)} %bitcast.59, bf16[1,384,1536]{2,1,0:T(8,128)(2,1)S(1)} %copy-done), kind=kOutput, calls=%fused_computation.9 | convolution fusion | flops 1517813760 | bytes 11993088 | tf_op jit(solution)/shard_map/dot_general | solution.py:510
  102.9 2.7 %fusion.3 = bf16[1,384,1536]{2,1,0:T(8,128)(2,1)} fusion(bf16[1280,384]{1,0:T(8,128)(2,1)S(1)} %get-tuple-element.34, bf16[1280,1536]{1,0:T(8,128)(2,1)S(1)} %bitcast.60), kind=kOutput, calls=%fused_computation.8 | convolution fusion | flops 1510539264 | bytes 6094848 | tf_op jit(solution)/shard_map/dot_general | solution.py:516
  105.6 3.3 %fusion.2 = bf16[1,1536,384]{2,1,0:T(8,128)(2,1)} fusion(bf16[1280,1536]{1,0:T(8,128)(2,1)S(1)} %bitcast.57, bf16[1280,384]{1,0:T(8,128)(2,1)S(1)} %get-tuple-element.32), kind=kOutput, calls=%fused_computation.7 | convolution fusion | flops 1510539264 | bytes 6094848 | tf_op jit(solution)/shard_map/dot_general | solution.py:516
  108.8 3.3 %fusion.1 = bf16[1,1536,384]{2,1,0:T(8,128)(2,1)} fusion(bf16[1280,1536]{1,0:T(8,128)(2,1)S(1)} %bitcast.58, bf16[1280,384]{1,0:T(8,128)(2,1)S(1)} %get-tuple-element.33), kind=kOutput, calls=%fused_computation.6 | convolution fusion | flops 1510539264 | bytes 6094848 | tf_op jit(solution)/shard_map/dot_general | solution.py:516
  112.1 4.3 %convolution_convert_fusion = bf16[1280,1536]{1,0:T(8,128)(2,1)} fusion(bf16[1280,384]{1,0:T(8,128)(2,1)S(1)} %get-tuple-element.34, bf16[1,384,1536]{2,1,0:T(8,128)(2,1)S(1)} %copy-done), kind=kOutput, calls=%fused_computation.2 | convolution fusion | flops 1511915520 | bytes 6094848 | tf_op jit(solution)/shard_map/dot_general | solution.py:506
  116.4 0.0 copy-start.2
  116.4 2.2 %fusion.10 = f32[1280,1536]{1,0:T(8,128)S(1)} fusion(bf16[1280,384]{1,0:T(8,128)(2,1)S(1)} %get-tuple-element.33, bf16[1,1536,384]{2,1,0:T(8,128)(2,1)S(1)} %copy-done.1), kind=kOutput, calls=%fused_computation.19 | convolution fusion | flops 1509949440 | bytes 10027008 | tf_op jit(solution)/shard_map/dot_general | solution.py:510
  118.7 0.0 copy-done.2
  118.7 4.2 %fusion = bf16[1280,1536]{1,0:T(8,128)(2,1)} fusion(f32[1280,1536]{1,0:T(8,128)S(1)} %fusion.10, bf16[1280,384]{1,0:T(8,128)(2,1)S(1)} %get-tuple-element.32, bf16[1,1536,384]{2,1,0:T(8,128)(2,1)S(1)} %copy-done.2), kind=kOutput, calls=%fused_computation.1 | convolution fusion | flops 1513881600 | bytes 13959168 | tf_op jit(solution)/shard_map/dot_general | solution.py:510
  122.9 92.2 %give_back.1 = (bf16[128,1536]{1,0:T(8,128)(2,1)}, bf16[128,1536]{1,0:T(8,128)(2,1)}, f32[128,128]{1,0:T(8,128)}) custom-call(bf16[4,8,40,1536]{3,2,1,0:T(8,128)(2,1)} %bitcast.52, bf16[4,8,40,1536]{3,2,1,0:T(8,128)(2,1)} %bitcast.51, bf16[4,128,1536]{2,1,0:T(8,128)(2,1)} %get-tuple-element.15.cot_group, f32[4,8,128]{2,1,0:T(8,128)} %get-tuple-element.16.meta_ref), custom_call_target="tpu_custom_call" | custom-call | tf_op jit(solution)/shard_map/give_back/pallas_call | solution.py:472
  215.1 1.5 copy.17
  216.6 1.8 copy.20
  218.3 1.8 copy.21
  (4 shorter events, 0.1 us)
Async XLA Ops:
  0.6 99.3 %copy-start = (bf16[1,384,1536]{2,1,0:T(8,128)(2,1)S(1)}, bf16[1,384,1536]{2,1,0:T(8,128)(2,1)}, u32[]{:S(2)}) copy-start(bf16[1,384,1536]{2,1,0:T(8,128)(2,1)} %param.12) | copy-start | bytes 3538948
  92.8 4.8 %copy-start.1 = (bf16[1,1536,384]{2,1,0:T(8,128)(2,1)S(1)}, bf16[1,1536,384]{2,1,0:T(8,128)(2,1)}, u32[]{:S(2)}) copy-start(bf16[1,1536,384]{2,1,0:T(8,128)(2,1)} %param.10) | copy-start | bytes 3538948
  92.9 4.8 %copy-start.3 = (bf16[4,8,40,1536]{3,2,1,0:T(8,128)(2,1)S(1)}, bf16[4,8,40,1536]{3,2,1,0:T(8,128)(2,1)}, u32[]{:S(2)}) copy-start(bf16[4,8,40,1536]{3,2,1,0:T(8,128)(2,1)} %get-tuple-element.13) | copy-start | bytes 11796484
  97.7 2.2 %copy-start.4 = (bf16[4,8,40,1536]{3,2,1,0:T(8,128)(2,1)S(1)}, bf16[4,8,40,1536]{3,2,1,0:T(8,128)(2,1)}, u32[]{:S(2)}) copy-start(bf16[4,8,40,1536]{3,2,1,0:T(8,128)(2,1)} %get-tuple-element.14) | copy-start | bytes 11796484
  116.4 2.3 %copy-start.2 = (bf16[1,1536,384]{2,1,0:T(8,128)(2,1)S(1)}, bf16[1,1536,384]{2,1,0:T(8,128)(2,1)}, u32[]{:S(2)}) copy-start(bf16[1,1536,384]{2,1,0:T(8,128)(2,1)} %param.11) | copy-start | bytes 3538948

commit v3 on v2

--- a/solution.py
+++ b/solution.py
@@ -41,15 +41,34 @@
     return rows == meta[0:1, :], rows == meta[1:2, :]
 
 
+def place(experts, capacity, meta_ref, meta_own):
+    count = meta_ref.shape[1]
+    meta = meta_ref[...]
+    names = lax.broadcasted_iota(jnp.int32, (experts, count), 0).astype(jnp.float32)
+    first = (names == meta[0:1, :]).astype(jnp.float32)
+    second = (names == meta[1:2, :]).astype(jnp.float32)
+    square = (count, count)
+    earlier = lax.broadcasted_iota(jnp.int32, square, 0) < lax.broadcasted_iota(jnp.int32, square, 1)
+    before = jnp.dot(
+        (first + second).astype(jnp.bfloat16),
+        earlier.astype(jnp.bfloat16),
+        preferred_element_type=jnp.float32,
+    )
+    meta_own[...] = meta
+    for k, chosen in enumerate((first, second)):
+        slot = jnp.sum(before * chosen, axis=0, keepdims=True)
+        meta_own[k : k + 1, :] = meta[k : k + 1, :] * capacity + slot
+
+
 def dispatch_kernel(
     groups, experts, capacity, tok_ref, cot_ref, meta_ref, tok_all, cot_all, cot_group, meta_all,
     landed, meta_in, staged, line_send, line_recv, plane_send, plane_recv, local_sem, keep_sem,
-    table_send, table_recv,
+    table_send, table_recv, meta_own,
 ):
     d = lax.axis_index("dp")
     e = lax.axis_index("expert")
     greet(groups, experts, d, e)
-    own = (tok_ref, cot_ref, meta_ref)
+    own = (tok_ref, cot_ref, meta_own)
     partner = d + 1 - 2 * lax.rem(d, 2)
     halves = split(tok_ref.shape[1])
     full = (tok_all, cot_all)
@@ -106,22 +125,25 @@
         return pltpu.make_async_copy(landed.at[1, s], cot_group.at[s], keep_sem.at[s])
 
     def process(a, s, source, meta_view):
-        def rows_of(other):
-            meta = meta_view[...]
-            first, second = picks(meta, other, capacity)
-            onehot = (first | second).astype(jnp.bfloat16)
-            rows = jnp.dot(onehot, source[...], preferred_element_type=jnp.float32)
+        meta = meta_view[...]
+        first, second = picks(meta, 0, experts * capacity)
+        onehot = (first | second).astype(jnp.bfloat16)
+        if a == 1:
+            weight = jnp.sum(
+                jnp.where(first, meta[2:3, :], 0.0) + jnp.where(second, meta[3:4, :], 0.0),
+                axis=1,
+                keepdims=True,
+            )
+        for half in halves:
+            rows = jnp.dot(onehot, source[:, half], preferred_element_type=jnp.float32)
             if a == 1:
-                weight = jnp.sum(
-                    jnp.where(first, meta[2:3, :], 0.0) + jnp.where(second, meta[3:4, :], 0.0),
-                    axis=1,
-                    keepdims=True,
-                )
                 rows = rows * weight
-            staged[a, s, other] = rows.astype(jnp.bfloat16)
+            for other in range(experts):
+                staged[a, s, other, :, half] = rows[
+                    other * capacity : (other + 1) * capacity
+                ].astype(jnp.bfloat16)
 
         def step(k, carry):
-            rows_of(lax.rem(e + k, experts))
             plane_copy(1, a, s, k).start()
 
             @pl.when(s != partner)
@@ -131,7 +153,6 @@
             return carry
 
         lax.fori_loop(1, experts, step, 0)
-        rows_of(e)
         local_copy(1, a, s).start()
 
         @pl.when(s != partner)
@@ -139,7 +160,9 @@
             local_copy(0, a, s).start()
 
     has_way = (d < groups - 1, d > 0)
-    for a in (2, 0, 1):
+    for a in (0, 1, 2):
+        if a == 2:
+            place(experts, capacity, meta_ref, meta_own)
         for way in (0, 1):
 
             @pl.when(has_way[way])
@@ -147,10 +170,10 @@
                 line_copy(a, d, way, 1, True).start()
 
     landed[1, d] = cot_ref[...]
-    meta_in[d] = meta_ref[...]
+    meta_in[d] = meta_own[...]
     keep_copy(d).start()
-    process(0, d, tok_ref, meta_ref)
-    process(1, d, cot_ref, meta_ref)
+    process(0, d, tok_ref, meta_own)
+    process(1, d, cot_ref, meta_own)
     for hop in range(1, groups):
         for way in (0, 1):
             s = d - hop + 2 * hop * way
@@ -256,6 +279,7 @@
             dma((groups,)),
             dma((2, experts)),
             dma((2, experts)),
+            pltpu.VMEM(meta.shape, meta.dtype),
         ],
         compiler_params=pltpu.CompilerParams(
             collective_id=0, has_side_effects=True, vmem_limit_bytes=56 << 20
@@ -372,11 +396,16 @@
         lax.fori_loop(0, experts, join, 0)
         send_rows(0, a, groups - 1)
 
-    def gathered(h, a, t, meta, which):
+    def gathered(h, a, t, meta, both):
         total = None
         for other in range(experts):
             first, second = picks(meta, other, capacity)
-            mask = (first, second, first | second)[which].astype(jnp.bfloat16)
+            if both:
+                mask = jnp.concatenate(
+                    [first.astype(jnp.bfloat16), second.astype(jnp.bfloat16)], axis=1
+                )
+            else:
+                mask = (first | second).astype(jnp.bfloat16)
             term = lax.dot_general(
                 mask,
                 landed[a, t, other, :, halves[h]],
@@ -389,15 +418,16 @@
     def gather_half(h, a, t, j):
         meta = meta_ref[j]
         if a == 1:
-            sums[1, j, :, halves[h]] = gathered(h, 1, t, meta, 2).astype(jnp.bfloat16)
+            sums[1, j, :, halves[h]] = gathered(h, 1, t, meta, False).astype(jnp.bfloat16)
             return
         lane = lax.broadcasted_iota(jnp.int32, (count, 128), 1)
         cot = cot_group[j, :, halves[h]].astype(jnp.float32)
         weights = jnp.transpose(meta)
         mixed = None
         dots = jnp.zeros((count, 128), jnp.float32)
+        pair = gathered(h, 0, t, meta, True)
         for which in (0, 1):
-            rows = gathered(h, 0, t, meta, which)
+            rows = pair[which * count : (which + 1) * count]
             dot = jnp.sum(cot * rows, axis=1, keepdims=True)
             dots = jnp.where(lane == which, dot, dots)
             term = weights[:, 2 + which : 3 + which] * rows
@@ -410,17 +440,25 @@
         j = target(t)
         for a in (0, 1):
 
-            @pl.when(j == partner)
-            def _(a=a, j=j):
-                sums[a, j, :, halves[0]] = jnp.zeros((count, halves[0].stop), sums.dtype)
-
-            @pl.when(j != partner)
-            def _(a=a, t=t, j=j):
-                await_rows(0, a, t)
-                gather_half(0, a, t, j)
-
-            await_rows(1, a, t)
-            gather_half(1, a, t, j)
+            if t == groups - 1:
+                if a == 0:
+                    for h in (1, 0):
+                        for c in (0, 1):
+                            await_rows(h, c, t)
+                            gather_half(h, c, t, j)
+            else:
+
+                @pl.when(j == partner)
+                def _(a=a, j=j):
+                    sums[a, j, :, halves[0]] = jnp.zeros((count, halves[0].stop), sums.dtype)
+
+                @pl.when(j != partner)
+                def _(a=a, t=t, j=j):
+                    await_rows(0, a, t)
+                    gather_half(0, a, t, j)
+
+                await_rows(1, a, t)
+                gather_half(1, a, t, j)
             for b in (0, 2) if a == 0 else (1,):
 
                 def add(way, b=b, j=j):
@@ -618,12 +656,8 @@
     capacity = 10 * count // (4 * experts)
     if capacity % 8 or count % 128 or width % 128 or width < 256 or groups % 2:
         return plain_device(tokens, routes, combine, w_gate, w_up, w_down, cotangent)
-    flat = routes.reshape(-1)
-    onehot = (flat[:, None] == jnp.arange(experts, dtype=jnp.int32)[None, :]).astype(jnp.int32)
-    before = jnp.cumsum(onehot, axis=0) - onehot
-    target_row = (flat * capacity + jnp.sum(before * onehot, axis=1)).reshape(count, 2)
     meta = jnp.concatenate(
-        [target_row.astype(jnp.float32).T, combine.T, jnp.zeros((4, count), jnp.float32)], axis=0
+        [routes.astype(jnp.float32).T, combine.T, jnp.zeros((4, count), jnp.float32)], axis=0
     )
     table = (groups, experts, capacity, width)
     tok_all, cot_all, cot_group, meta_all = dispatch(

time: 220 us -> 218 us (level)
    unnamed x14 -> x13, local copies, waits for them, and re-layouts: 5.9 us -> 5.04 us
where the time goes in v3:
time: 218 us; the launch traced here: 217 us
  Pallas kernels  180 us (83%)
  matrix products  29.9 us (14%)
  local copies, waits for them, and re-layouts  5.11 us (2%)
    pallas_call x1, Pallas kernels, give_back(): pl.pallas_call(functools.partial(return_kernel, groups, experts, capacity...  92 us
    pallas_call x1, Pallas kernels, dispatch(): pl.pallas_call(functools.partial(dispatch_kernel, groups, experts, capaci...  87.6 us
    dot_general x3, matrix products, dot_plain(): return jnp.dot(left, right, preferred_element_type=jnp.float32)  11.3 us
    dot_general x3, matrix products, dot_last(): lax.dot_general(left, right, (((1,), (1,)), ((), ())), preferred_element_...  9.33 us
    dot_general x3, matrix products, dot_first(): lax.dot_general(left, right, (((0,), (0,)), ((), ())), preferred_element_...  9.24 us
    unnamed x13, local copies, waits for them, and re-layouts  5.04 us

profile of v3, /device:TPU:0, one launch (start us, length us, event | category | flops | bytes accessed | tf_op | source)
XLA Modules:
  0.0 217.4 jit_solution(5509265679037525848)
XLA Ops:
  0.6 0.0 copy-start
  0.7 0.1 pad.2.clone
  0.7 0.8 convert_bitcast_fusion
  1.5 1.3 maximum_maximum_fusion.meta_ref
  2.8 87.6 %dispatch.1 = (bf16[4,8,40,1536]{3,2,1,0:T(8,128)(2,1)}, bf16[4,8,40,1536]{3,2,1,0:T(8,128)(2,1)}, bf16[4,128,1536]{2,1,0:T(8,128)(2,1)}, f32[4,8,128]{2,1,0:T(8,128)}) custom-call(bf16[128,1536]{1,0:T(8,128)(2,1)} %tok_ref.1, bf16[128,1536]{1,0:T(8,128)(2,1)} %cot_ref.1, f32[8,128]{1,0:T(8,128)} %maximum_maximum_fusion.meta_ref), custom_call_target="tpu_custom_call" | custom-call | tf_op jit(solution)/shard_map/dispatch/pallas_call | solution.py:260
  90.4 0.0 copy-start.1
  90.4 0.0 copy-start.3
  90.4 4.8 %fusion.8 = f32[1280,384]{1,0:T(8,128)S(1)} fusion(bf16[1280,1536]{1,0:T(8,128)(2,1)} %bitcast.47, bf16[1,1536,384]{2,1,0:T(8,128)(2,1)} %param.11), kind=kOutput, calls=%fused_computation.17 | convolution fusion | flops 1509949440 | bytes 7077888 | tf_op jit(solution)/shard_map/dot_general | solution.py:544
  95.3 0.0 copy-done.1
  95.3 0.0 copy-done.3
  95.3 0.0 copy-start.4
  95.3 2.2 %fusion.12 = f32[1280,384]{1,0:T(8,128)S(1)} fusion(bf16[1280,1536]{1,0:T(8,128)(2,1)S(1)} %bitcast.48, bf16[1,1536,384]{2,1,0:T(8,128)(2,1)S(1)} %copy-done.1), kind=kOutput, calls=%fused_computation.21 | convolution fusion | flops 1509949440 | bytes 7077888 | tf_op jit(solution)/shard_map/dot_general | solution.py:544
  97.5 0.0 copy-done
  97.5 0.0 copy-done.4
  97.5 2.9 %multiply_convert_fusion = (bf16[1280,384]{1,0:T(8,128)(2,1)S(1)}, bf16[1280,384]{1,0:T(8,128)(2,1)S(1)}, bf16[1280,384]{1,0:T(8,128)(2,1)S(1)}) fusion(f32[1280,384]{1,0:T(8,128)S(1)} %fusion.12, f32[1280,384]{1,0:T(8,128)S(1)} %fusion.8, bf16[1280,1536]{1,0:T(8,128)(2,1)S(1)} %bitcast.51, bf16[1,384,1536]{2,1,0:T(8,128)(2,1)S(1)} %copy-done), kind=kOutput, calls=%fused_computation.9 | convolution fusion | flops 1517813760 | bytes 11993088 | tf_op jit(solution)/shard_map/dot_general | solution.py:548
  100.4 2.7 %fusion.3 = bf16[1,384,1536]{2,1,0:T(8,128)(2,1)} fusion(bf16[1280,384]{1,0:T(8,128)(2,1)S(1)} %get-tuple-element.28, bf16[1280,1536]{1,0:T(8,128)(2,1)S(1)} %bitcast.52), kind=kOutput, calls=%fused_computation.8 | convolution fusion | flops 1510539264 | bytes 6094848 | tf_op jit(solution)/shard_map/dot_general | solution.py:554
  103.2 3.3 %fusion.2 = bf16[1,1536,384]{2,1,0:T(8,128)(2,1)} fusion(bf16[1280,1536]{1,0:T(8,128)(2,1)S(1)} %bitcast.49, bf16[1280,384]{1,0:T(8,128)(2,1)S(1)} %get-tuple-element.26), kind=kOutput, calls=%fused_computation.7 | convolution fusion | flops 1510539264 | bytes 6094848 | tf_op jit(solution)/shard_map/dot_general | solution.py:554
  106.4 3.3 %fusion.1 = bf16[1,1536,384]{2,1,0:T(8,128)(2,1)} fusion(bf16[1280,1536]{1,0:T(8,128)(2,1)S(1)} %bitcast.50, bf16[1280,384]{1,0:T(8,128)(2,1)S(1)} %get-tuple-element.27), kind=kOutput, calls=%fused_computation.6 | convolution fusion | flops 1510539264 | bytes 6094848 | tf_op jit(solution)/shard_map/dot_general | solution.py:554
  109.7 4.3 %convolution_convert_fusion = bf16[1280,1536]{1,0:T(8,128)(2,1)} fusion(bf16[1280,384]{1,0:T(8,128)(2,1)S(1)} %get-tuple-element.28, bf16[1,384,1536]{2,1,0:T(8,128)(2,1)S(1)} %copy-done), kind=kOutput, calls=%fused_computation.2 | convolution fusion | flops 1511915520 | bytes 6094848 | tf_op jit(solution)/shard_map/dot_general | solution.py:544
  114.0 0.0 copy-start.2
  114.0 2.2 %fusion.10 = f32[1280,1536]{1,0:T(8,128)S(1)} fusion(bf16[1280,384]{1,0:T(8,128)(2,1)S(1)} %get-tuple-element.27, bf16[1,1536,384]{2,1,0:T(8,128)(2,1)S(1)} %copy-done.1), kind=kOutput, calls=%fused_computation.19 | convolution fusion | flops 1509949440 | bytes 10027008 | tf_op jit(solution)/shard_map/dot_general | solution.py:548
  116.2 0.0 copy-done.2
  116.3 4.2 %fusion = bf16[1280,1536]{1,0:T(8,128)(2,1)} fusion(f32[1280,1536]{1,0:T(8,128)S(1)} %fusion.10, bf16[1280,384]{1,0:T(8,128)(2,1)S(1)} %get-tuple-element.26, bf16[1,1536,384]{2,1,0:T(8,128)(2,1)S(1)} %copy-done.2), kind=kOutput, calls=%fused_computation.1 | convolution fusion | flops 1513881600 | bytes 13959168 | tf_op jit(solution)/shard_map/dot_general | solution.py:548
  120.4 92.0 %give_back.1 = (bf16[128,1536]{1,0:T(8,128)(2,1)}, bf16[128,1536]{1,0:T(8,128)(2,1)}, f32[128,128]{1,0:T(8,128)}) custom-call(bf16[4,8,40,1536]{3,2,1,0:T(8,128)(2,1)} %bitcast.44, bf16[4,8,40,1536]{3,2,1,0:T(8,128)(2,1)} %bitcast.43, bf16[4,128,1536]{2,1,0:T(8,128)(2,1)} %get-tuple-element.15.cot_group, f32[4,8,128]{2,1,0:T(8,128)} %get-tuple-element.16.meta_ref), custom_call_target="tpu_custom_call" | custom-call | tf_op jit(solution)/shard_map/give_back/pallas_call | solution.py:510
  212.4 1.5 copy.13
  213.9 1.8 copy.16
  215.6 1.8 copy.17
  (1 shorter events, 0.0 us)
Async XLA Ops:
  0.6 96.9 %copy-start = (bf16[1,384,1536]{2,1,0:T(8,128)(2,1)S(1)}, bf16[1,384,1536]{2,1,0:T(8,128)(2,1)}, u32[]{:S(2)}) copy-start(bf16[1,384,1536]{2,1,0:T(8,128)(2,1)} %param.12) | copy-start | bytes 3538948
  90.4 4.8 %copy-start.1 = (bf16[1,1536,384]{2,1,0:T(8,128)(2,1)S(1)}, bf16[1,1536,384]{2,1,0:T(8,128)(2,1)}, u32[]{:S(2)}) copy-start(bf16[1,1536,384]{2,1,0:T(8,128)(2,1)} %param.10) | copy-start | bytes 3538948
  90.4 4.8 %copy-start.3 = (bf16[4,8,40,1536]{3,2,1,0:T(8,128)(2,1)S(1)}, bf16[4,8,40,1536]{3,2,1,0:T(8,128)(2,1)}, u32[]{:S(2)}) copy-start(bf16[4,8,40,1536]{3,2,1,0:T(8,128)(2,1)} %get-tuple-element.13) | copy-start | bytes 11796484
  95.3 2.2 %copy-start.4 = (bf16[4,8,40,1536]{3,2,1,0:T(8,128)(2,1)S(1)}, bf16[4,8,40,1536]{3,2,1,0:T(8,128)(2,1)}, u32[]{:S(2)}) copy-start(bf16[4,8,40,1536]{3,2,1,0:T(8,128)(2,1)} %get-tuple-element.14) | copy-start | bytes 11796484
  114.0 2.3 %copy-start.2 = (bf16[1,1536,384]{2,1,0:T(8,128)(2,1)S(1)}, bf16[1,1536,384]{2,1,0:T(8,128)(2,1)}, u32[]{:S(2)}) copy-start(bf16[1,1536,384]{2,1,0:T(8,128)(2,1)} %param.11) | copy-start | bytes 3538948

commit v4 on v3

--- a/solution.py
+++ b/solution.py
@@ -30,7 +30,7 @@
 
 
 def split(width):
-    half = width // 256 * 128
+    half = width // 384 * 128
     return (slice(0, half), slice(half, width))
 
 
@@ -499,6 +499,28 @@
             @pl.when(j < d)
             def _(b=b, j=j):
                 line_copy(b, j, 1).wait_send()
+
+
+def finish_kernel(out_in, back_in, dots_in, out_ref, back_ref, dots_ref):
+    out_ref[...] = out_in[...]
+    back_ref[...] = back_in[...]
+    dots_ref[...] = jnp.transpose(dots_in[...])[: dots_ref.shape[0]]
+
+
+def finish(out, back, dots):
+    vmem = pl.BlockSpec(memory_space=pltpu.VMEM)
+    out, back, dots = pl.pallas_call(
+        finish_kernel,
+        out_shape=(
+            jax.ShapeDtypeStruct(out.shape, out.dtype),
+            jax.ShapeDtypeStruct(back.shape, back.dtype),
+            jax.ShapeDtypeStruct((2, out.shape[0]), dots.dtype),
+        ),
+        in_specs=[vmem] * 3,
+        out_specs=(vmem,) * 3,
+        name="finish",
+    )(out, back, dots)
+    return out, back, dots.T
 
 
 def give_back(groups, experts, capacity, out_rows, back_rows, cot_group, meta_all):
@@ -654,7 +676,7 @@
     groups = lax.axis_size("dp")
     count, width = tokens.shape
     capacity = 10 * count // (4 * experts)
-    if capacity % 8 or count % 128 or width % 128 or width < 256 or groups % 2:
+    if capacity % 8 or count % 128 or width % 128 or width < 384 or groups % 2:
         return plain_device(tokens, routes, combine, w_gate, w_up, w_down, cotangent)
     meta = jnp.concatenate(
         [routes.astype(jnp.float32).T, combine.T, jnp.zeros((4, count), jnp.float32)], axis=0
@@ -680,10 +702,11 @@
         groups, experts, capacity, out_part.reshape(table), back_part.reshape(table),
         cot_group, meta_all,
     )
+    out, d_tokens, d_combine = finish(out, d_tokens, dots)
     grad_gate = dot_first(group_rows, d_gate).astype(jnp.bfloat16)
     grad_up = dot_first(group_rows, d_up).astype(jnp.bfloat16)
     grad_down = dot_first(hidden, group_cot).astype(jnp.bfloat16)
-    return (out, d_tokens, dots[:, :2], grad_gate[None], grad_up[None], grad_down[None])
+    return (out, d_tokens, d_combine, grad_gate[None], grad_up[None], grad_down[None])
 
 
 def solution(mesh):

time: 218 us -> 211 us (0.968)
  local copies, waits for them, and re-layouts: 5.11 us -> 0.11 us
    unnamed x13 -> x10, local copies, waits for them, and re-layouts: 5.04 us -> 0.03 us
    pallas_call x1, Pallas kernels: 92 us -> 87.9 us  [give_back(): pl.pallas_call(functools.partial(return_kernel, groups, experts, capacity...]
where the time goes in v4:
time: 211 us; the launch traced here: 210 us
  Pallas kernels  178 us (84%)
  matrix products  29.9 us (14%)
    pallas_call x1, Pallas kernels, give_back(): pl.pallas_call(functools.partial(return_kernel, groups, experts, capacity...  87.9 us
    pallas_call x1, Pallas kernels, dispatch(): pl.pallas_call(functools.partial(dispatch_kernel, groups, experts, capaci...  87.7 us
    dot_general x3, matrix products, dot_plain(): return jnp.dot(left, right, preferred_element_type=jnp.float32)  11.3 us
    dot_general x3, matrix products, dot_last(): lax.dot_general(left, right, (((1,), (1,)), ((), ())), preferred_element_...  9.33 us
    dot_general x3, matrix products, dot_first(): lax.dot_general(left, right, (((0,), (0,)), ((), ())), preferred_element_...  9.24 us

profile of v4, /device:TPU:0, one launch (start us, length us, event | category | flops | bytes accessed | tf_op | source)
XLA Modules:
  0.0 210.5 jit_solution(17917603083810469705)
XLA Ops:
  0.6 0.0 copy-start
  0.7 0.1 pad.2.clone
  0.7 0.8 convert_bitcast_fusion
  1.5 1.3 maximum_maximum_fusion.meta_ref
  2.8 87.7 %dispatch.1 = (bf16[4,8,40,1536]{3,2,1,0:T(8,128)(2,1)}, bf16[4,8,40,1536]{3,2,1,0:T(8,128)(2,1)}, bf16[4,128,1536]{2,1,0:T(8,128)(2,1)}, f32[4,8,128]{2,1,0:T(8,128)}) custom-call(bf16[128,1536]{1,0:T(8,128)(2,1)} %tok_ref.1, bf16[128,1536]{1,0:T(8,128)(2,1)} %cot_ref.1, f32[8,128]{1,0:T(8,128)} %maximum_maximum_fusion.meta_ref), custom_call_target="tpu_custom_call" | custom-call | tf_op jit(solution)/shard_map/dispatch/pallas_call | solution.py:260
  90.5 0.0 copy-start.1
  90.5 0.0 copy-start.3
  90.5 4.8 %fusion.8 = f32[1280,384]{1,0:T(8,128)S(1)} fusion(bf16[1280,1536]{1,0:T(8,128)(2,1)} %bitcast.46, bf16[1,1536,384]{2,1,0:T(8,128)(2,1)} %param.11), kind=kOutput, calls=%fused_computation.17 | convolution fusion | flops 1509949440 | bytes 7077888 | tf_op jit(solution)/shard_map/dot_general | solution.py:566
  95.3 0.0 copy-done.1
  95.4 0.0 copy-done.3
  95.4 0.0 copy-start.4
  95.4 2.2 %fusion.12 = f32[1280,384]{1,0:T(8,128)S(1)} fusion(bf16[1280,1536]{1,0:T(8,128)(2,1)S(1)} %bitcast.47, bf16[1,1536,384]{2,1,0:T(8,128)(2,1)S(1)} %copy-done.1), kind=kOutput, calls=%fused_computation.21 | convolution fusion | flops 1509949440 | bytes 7077888 | tf_op jit(solution)/shard_map/dot_general | solution.py:566
  97.6 0.0 copy-done
  97.6 0.0 copy-done.4
  97.6 2.9 %multiply_convert_fusion = (bf16[1280,384]{1,0:T(8,128)(2,1)S(1)}, bf16[1280,384]{1,0:T(8,128)(2,1)S(1)}, bf16[1280,384]{1,0:T(8,128)(2,1)S(1)}) fusion(f32[1280,384]{1,0:T(8,128)S(1)} %fusion.12, f32[1280,384]{1,0:T(8,128)S(1)} %fusion.8, bf16[1280,1536]{1,0:T(8,128)(2,1)S(1)} %bitcast.50, bf16[1,384,1536]{2,1,0:T(8,128)(2,1)S(1)} %copy-done), kind=kOutput, calls=%fused_computation.9 | convolution fusion | flops 1517813760 | bytes 11993088 | tf_op jit(solution)/shard_map/dot_general | solution.py:570
  100.5 2.7 %fusion.3 = bf16[1,384,1536]{2,1,0:T(8,128)(2,1)} fusion(bf16[1280,384]{1,0:T(8,128)(2,1)S(1)} %get-tuple-element.28, bf16[1280,1536]{1,0:T(8,128)(2,1)S(1)} %bitcast.51), kind=kOutput, calls=%fused_computation.8 | convolution fusion | flops 1510539264 | bytes 6094848 | tf_op jit(solution)/shard_map/dot_general | solution.py:576
  103.3 3.3 %fusion.2 = bf16[1,1536,384]{2,1,0:T(8,128)(2,1)} fusion(bf16[1280,1536]{1,0:T(8,128)(2,1)S(1)} %bitcast.48, bf16[1280,384]{1,0:T(8,128)(2,1)S(1)} %get-tuple-element.26), kind=kOutput, calls=%fused_computation.7 | convolution fusion | flops 1510539264 | bytes 6094848 | tf_op jit(solution)/shard_map/dot_general | solution.py:576
  106.5 3.3 %fusion.1 = bf16[1,1536,384]{2,1,0:T(8,128)(2,1)} fusion(bf16[1280,1536]{1,0:T(8,128)(2,1)S(1)} %bitcast.49, bf16[1280,384]{1,0:T(8,128)(2,1)S(1)} %get-tuple-element.27), kind=kOutput, calls=%fused_computation.6 | convolution fusion | flops 1510539264 | bytes 6094848 | tf_op jit(solution)/shard_map/dot_general | solution.py:576
  109.8 4.3 %convolution_convert_fusion = bf16[1280,1536]{1,0:T(8,128)(2,1)} fusion(bf16[1280,384]{1,0:T(8,128)(2,1)S(1)} %get-tuple-element.28, bf16[1,384,1536]{2,1,0:T(8,128)(2,1)S(1)} %copy-done), kind=kOutput, calls=%fused_computation.2 | convolution fusion | flops 1511915520 | bytes 6094848 | tf_op jit(solution)/shard_map/dot_general | solution.py:566
  114.1 0.0 copy-start.2
  114.1 2.2 %fusion.10 = f32[1280,1536]{1,0:T(8,128)S(1)} fusion(bf16[1280,384]{1,0:T(8,128)(2,1)S(1)} %get-tuple-element.27, bf16[1,1536,384]{2,1,0:T(8,128)(2,1)S(1)} %copy-done.1), kind=kOutput, calls=%fused_computation.19 | convolution fusion | flops 1509949440 | bytes 10027008 | tf_op jit(solution)/shard_map/dot_general | solution.py:570
  116.3 0.0 copy-done.2
  116.3 4.1 %fusion = bf16[1280,1536]{1,0:T(8,128)(2,1)} fusion(f32[1280,1536]{1,0:T(8,128)S(1)} %fusion.10, bf16[1280,384]{1,0:T(8,128)(2,1)S(1)} %get-tuple-element.26, bf16[1,1536,384]{2,1,0:T(8,128)(2,1)S(1)} %copy-done.2), kind=kOutput, calls=%fused_computation.1 | convolution fusion | flops 1513881600 | bytes 13959168 | tf_op jit(solution)/shard_map/dot_general | solution.py:570
  120.5 87.9 %give_back.1 = (bf16[128,1536]{1,0:T(8,128)(2,1)}, bf16[128,1536]{1,0:T(8,128)(2,1)}, f32[128,128]{1,0:T(8,128)}) custom-call(bf16[4,8,40,1536]{3,2,1,0:T(8,128)(2,1)} %bitcast.44, bf16[4,8,40,1536]{3,2,1,0:T(8,128)(2,1)} %bitcast.43, bf16[4,128,1536]{2,1,0:T(8,128)(2,1)} %get-tuple-element.18.cot_group, f32[4,8,128]{2,1,0:T(8,128)} %get-tuple-element.19.meta_ref), custom_call_target="tpu_custom_call" | custom-call | tf_op jit(solution)/shard_map/give_back/pallas_call | solution.py:532
  208.5 2.0 finish.1
  (1 shorter events, 0.0 us)
Async XLA Ops:
  0.6 96.9 %copy-start = (bf16[1,384,1536]{2,1,0:T(8,128)(2,1)S(1)}, bf16[1,384,1536]{2,1,0:T(8,128)(2,1)}, u32[]{:S(2)}) copy-start(bf16[1,384,1536]{2,1,0:T(8,128)(2,1)} %param.12) | copy-start | bytes 3538948
  90.5 4.8 %copy-start.1 = (bf16[1,1536,384]{2,1,0:T(8,128)(2,1)S(1)}, bf16[1,1536,384]{2,1,0:T(8,128)(2,1)}, u32[]{:S(2)}) copy-start(bf16[1,1536,384]{2,1,0:T(8,128)(2,1)} %param.10) | copy-start | bytes 3538948
  90.5 4.8 %copy-start.3 = (bf16[4,8,40,1536]{3,2,1,0:T(8,128)(2,1)S(1)}, bf16[4,8,40,1536]{3,2,1,0:T(8,128)(2,1)}, u32[]{:S(2)}) copy-start(bf16[4,8,40,1536]{3,2,1,0:T(8,128)(2,1)} %get-tuple-element.16) | copy-start | bytes 11796484
  95.4 2.2 %copy-start.4 = (bf16[4,8,40,1536]{3,2,1,0:T(8,128)(2,1)S(1)}, bf16[4,8,40,1536]{3,2,1,0:T(8,128)(2,1)}, u32[]{:S(2)}) copy-start(bf16[4,8,40,1536]{3,2,1,0:T(8,128)(2,1)} %get-tuple-element.17) | copy-start | bytes 11796484
  114.1 2.3 %copy-start.2 = (bf16[1,1536,384]{2,1,0:T(8,128)(2,1)S(1)}, bf16[1,1536,384]{2,1,0:T(8,128)(2,1)}, u32[]{:S(2)}) copy-start(bf16[1,1536,384]{2,1,0:T(8,128)(2,1)} %param.11) | copy-start | bytes 3538948
